TPU v7x, 32 devices: a whole 2x2x4 slice. The times are simulated.
32 devices in a mesh: row: 4 (over x, core), col: 8 (over z, y).
Axes of the slice: x: 2, y: 2, z: 4, core: 2. Of those that a mesh axis runs over, the one named last changes fastest.
Arguments:
- rhs: float32 [32768, 512], P('col', 'row'), may hold values from -6 to 6
- factors: bfloat16 [32768, 2048], P('col', 'row'), may hold values from -0.15625 to 0.15625
- diag_inv: float32 [4, 512, 512], replicated, may hold values from -2 to 2, as said below
Outputs:
- solution: float32 [32768, 512], P('col', 'row')
Inputs may be any that keep to these rules, and one draw needn't show every extreme that they name: `diag_inv`: entries off the diagonal of each block lie within 2 / sqrt(512) in magnitude; diagonal entries lie in 0.5 to 2.
All inputs are finite; a program needn't handle non-finite values.
Results may differ from a plain program's by a relative error of at most 0.0038.
Values may be sent and summed in bfloat16 or wider, within the bound.
A program may use at most 128 MiB of HBM per device.

v0:
```python
import functools

import jax
import jax.numpy as jnp
from jax import lax
from jax.experimental import pallas as pl
from jax.experimental.pallas import tpu as pltpu
from jax.sharding import PartitionSpec as P

MESH = pl.DeviceIdType.MESH
F32 = jnp.float32
BF16 = jnp.bfloat16
CHUNKS = 8
PARTS = 4
GATHER = 3


def remote(src, dst, send_sem, recv_sem, **device):
    return pltpu.make_async_remote_copy(
        src_ref=src,
        dst_ref=dst,
        send_sem=send_sem,
        recv_sem=recv_sem,
        device_id=device,
        device_id_type=MESH,
    )


def dot(a, b):
    return jnp.dot(a, b, preferred_element_type=F32)


def split(value):
    high = value.astype(BF16)
    return high, (value - high.astype(F32)).astype(BF16)


def kernel(
    n_row, n_col, steps, block,
    rhs_hbm, factors_hbm, diag_ref, out_ref,
    rhs_ref, factors_ref, extra,
    diag, low_hi, low_lo, up_hi, up_lo, panel, solved, last, work, gathered,
    send1, recv1, own1, send2, recv2,
    diag_sem, f_send, f_recv, f_fwd, s_chain, s_side, s_row, s_recv, s_last, g_local, g_recv,
    one_send, one_recv, two_send, two_recv, x_send, x_recv, x_fwd, load_sem,
):
    rows_dev, width = rhs_hbm.shape
    cols = factors_ref.shape[1]
    pieces = block // cols
    chips = n_row // 2
    side = n_col // steps
    row = lax.axis_index("row")
    col = lax.axis_index("col")
    chip, core = row // 2, row % 2
    sibling = chip * 2 + 1 - core
    zone, lane = col // side, col % side
    owner = lane == 0
    base = zone * side

    diag_copy = pltpu.make_async_copy(diag_ref.at[zone], diag, diag_sem)
    rhs_copy = pltpu.make_async_copy(rhs_hbm.at[pl.ds(0, block)], rhs_ref, load_sem.at[0])
    factors_copy = pltpu.make_async_copy(factors_hbm, factors_ref, load_sem.at[1])
    work_copy = pltpu.make_async_copy(rhs_hbm.at[pl.ds(0, block)], work, load_sem.at[2])
    panel_own = pltpu.make_async_copy(factors_hbm.at[pl.ds(0, block)], panel.at[row], load_sem.at[3])
    diag_copy.start()
    work_copy.start()
    panel_own.start()
    factors_copy.start()
    rhs_copy.start()

    barrier = pltpu.get_barrier_semaphore()
    for d in range(1, n_row):
        pl.semaphore_signal(barrier, inc=1, device_id={"row": (row + d) % n_row}, device_id_type=MESH)
    for d in range(1, n_col):
        pl.semaphore_signal(barrier, inc=1, device_id={"col": (col + d) % n_col}, device_id_type=MESH)
    pl.semaphore_wait(barrier, n_row + n_col - 2)

    window = factors_hbm.at[pl.ds(0, block)]
    far = [((chip + d) % chips) * 2 + core for d in range(1, chips)]
    sends_panel = jnp.logical_and(owner, row // pieces != zone)

    def panel_copy(d):
        return remote(window, panel.at[row], f_send.at[d], f_recv.at[row], row=far[d - 1] if d else sibling)

    @pl.when(sends_panel)
    def _():
        for d in list(range(1, chips)) + [0]:
            panel_copy(d).start()

    step_rows = rows_dev // CHUNKS
    n_extra = jnp.maximum(GATHER - (zone + 1) // 2 - jnp.where(owner, 1, 0), 0)

    def span(m):
        return pl.ds(pl.multiple_of(m * step_rows, step_rows), step_rows)

    def extra_copy(g, d):
        return remote(
            factors_hbm.at[span(CHUNKS - 1 - g)], extra.at[g, row], x_send.at[g, d], x_recv.at[g, row],
            row=far[d - 1] if d else sibling,
        )

    def extra_forward(g, source):
        return remote(extra.at[g, source], extra.at[g, source], x_fwd.at[g, source // 2], x_recv.at[g, source], row=sibling)

    def extra_start(g, carry):
        for d in range(chips):
            extra_copy(g, d).start()
        return carry

    waits = jnp.logical_and(owner, zone > 0)
    lax.fori_loop(0, jnp.where(waits, 0, n_extra), extra_start, 0)
    diag_copy.wait()
    work_copy.wait()
    panel_own.wait()

    @pl.when(owner)
    def _():
        down = lax.broadcasted_iota(jnp.int32, (block, block), 0)
        across = lax.broadcasted_iota(jnp.int32, (block, block), 1)
        matrix = diag[...]
        low_hi[...], low_lo[...] = split(jnp.where(down > across, matrix, 0.0))
        up_hi[...], up_lo[...] = split(jnp.where(down <= across, matrix, 0.0))

    part_rows = block // PARTS

    def part(q):
        return pl.ds(q * part_rows, part_rows)

    def solve(hi, lo, high, low, q):
        return dot(hi[part(q)], high) + (dot(hi[part(q)], low) + dot(lo[part(q)], high))

    def forward_piece(source):
        return remote(panel.at[source], panel.at[source], f_fwd.at[source // 2], f_recv.at[source], row=sibling)

    def slot(t):
        return jnp.where(t <= zone, t, steps + zone - t)

    def hand_on(t):
        if t == steps:
            return
        for p in range(pieces):
            source = slot(t) * pieces + p
            here = jnp.logical_and(owner, t != zone)

            @pl.when(here & (source != row) & (source % 2 == core))
            def _():
                forward_piece(source).wait_recv()
                forward_piece(source).start()

    def arrive_panel(j):
        for p in range(pieces):
            source = j * pieces + p

            @pl.when(source % 2 != core)
            def _():
                forward_piece(source).wait_recv()

    def chain_copy(t, j, q):
        target = jnp.where(t <= zone, zone + 1, zone - 1)
        piece = solved.at[j, part(q)]
        return remote(piece, piece, s_chain.at[t, q], s_recv.at[j, q], col=target * side)

    def chain_sends(t):
        return jnp.where(t <= zone, zone < steps - 1, zone > 0)

    def side_copy(t, j, d, q):
        piece = solved.at[j, part(q)]
        return remote(piece, piece, s_side.at[t, d, q], s_recv.at[j, q], col=base + d)

    def pass_on(t, j, q):
        @pl.when(jnp.logical_and(owner, chain_sends(t)))
        def _():
            chain_copy(t, j, q).start()

        @pl.when(owner)
        def _():
            for d in range(1, side):
                side_copy(t, j, d, q).start()

    def update(j, q):
        first_row = (q - 1) * part_rows
        total = work[...]
        depth = min(2 * part_rows, cols)
        for start in range(first_row, first_row + 2 * part_rows, depth):
            total = total - dot(
                panel[j * pieces + start // cols, :, pl.ds(start % cols, depth)],
                solved[j, pl.ds(start, depth)],
            )
        work[...] = total

    per = PARTS // pieces
    my_columns = pl.ds(pl.multiple_of(chip * width, width), width)

    def row_copy(t, j, q):
        return remote(
            solved.at[j, part(q)], gathered.at[core, part(q % per), my_columns],
            s_row.at[t, q], g_recv.at[row, q % per], row=j * pieces + q // per,
        )

    def local_copy(j, q):
        return pltpu.make_async_copy(
            solved.at[j, part(q)], gathered.at[core, part(q % per), my_columns], g_local.at[q % per]
        )

    def share(t, j, q):
        @pl.when(j * pieces + q // per != row)
        def _():
            row_copy(t, j, q).start()

        @pl.when(j * pieces + q // per == row)
        def _():
            local_copy(j, q).start()

    def one_copy(m):
        return remote(send1.at[m], recv1.at[m], one_send.at[m], one_recv.at[m], row=sibling)

    def two_copy(m, d):
        return remote(send2.at[m, d - 1], recv2.at[m, d - 1], two_send.at[m, d - 1], two_recv.at[m, d - 1], row=far[d - 1])

    def first(m, carry):
        send1[m] = dot(factors_ref[span(m)], gathered[1 - core]).astype(BF16)
        one_copy(m).start()
        return carry

    def second(m, carry):
        @pl.when(m + 1 < n_swap)
        def _():
            first(m + 1, 0)

        own1[m] = dot(factors_ref[span(m)], gathered[core])
        one_copy(m).wait_recv()
        for d in range(1, chips):
            there = pl.ds(pl.multiple_of(((chip + d) % chips) * width, width), width)
            send2[m, d - 1] = (own1[m, :, there] + recv1[m, :, there].astype(F32)).astype(BF16)
            two_copy(m, d).start()
        return carry

    def third(m, carry):
        here = pl.ds(pl.multiple_of(chip * width, width), width)
        total = own1[m, :, here] + recv1[m, :, here].astype(F32)
        for d in range(1, chips):
            two_copy(m, d).wait_recv()
            total = total + recv2[m, d - 1].astype(F32)
        out_ref[span(m)] = total
        return carry

    def finish(m, carry):
        one_copy(m).wait_send()
        for d in range(1, chips):
            two_copy(m, d).wait_send()
        return carry

    n_swap = CHUNKS - n_extra

    def extra_hand_on(g, carry):
        for d in range(1, chips):
            extra_forward(g, far[d - 1]).wait_recv()
            extra_forward(g, far[d - 1]).start()
        return carry

    def extra_product(g, carry):
        rows = span(CHUNKS - 1 - g)
        total = jnp.zeros((step_rows, width), F32)
        for d in range(n_row):
            source = (row + d) % n_row
            part_of = solved[source // pieces, pl.ds(pl.multiple_of((source % pieces) * cols, cols), cols)]
            if d == 0:
                total = total + dot(factors_ref[rows], part_of)
            else:
                @pl.when(source % 2 != core)
                def _():
                    extra_forward(g, source).wait_recv()

                total = total + dot(extra[g, source], part_of)
        out_ref[rows] = total
        return carry

    def extra_finish(g, carry):
        for d in range(chips):
            extra_copy(g, d).wait_send()
        for d in range(1, chips):
            extra_forward(g, far[d - 1]).wait_send()
        return carry

    def first_products():
        factors_copy.wait()
        rhs_copy.wait()
        for q in range(per):
            local_copy(0, q).wait()
        for d in range(1, n_row):
            source = (row + d) % n_row
            for q in range(per):
                piece = gathered.at[source % 2, part(q), pl.ds(pl.multiple_of((source // 2) * width, width), width)]
                remote(piece, piece, g_local.at[q], g_recv.at[source, q], row=source).wait_recv()
        first(0, 0)

    for t in range(steps):
        j = slot(t)
        mine = jnp.logical_and(owner, t == zone)
        if t == 0:
            hand_on(t)

        @pl.when(jnp.logical_and(owner, t != zone))
        def _():
            arrive_panel(j)

        @pl.when(mine)
        def _():
            high, low = split(work[...])
            for q in range(PARTS):
                value = work[part(q)] + solve(low_hi, low_lo, high, low, q)
                work[part(q)] = value
                solved[j, part(q)] = value.astype(BF16)
                pass_on(t, j, q)
                share(t, j, q)

        @pl.when(jnp.logical_not(mine))
        def _():
            for q in range(PARTS):
                chain_copy(t, j, q).wait_recv()
                pass_on(t, j, q)
                share(t, j, q)
                if q % 2:
                    @pl.when(owner)
                    def _():
                        update(j, q)

        hand_on(t + 1)
        if t == 0:
            lax.fori_loop(0, jnp.where(waits, n_extra, 0), extra_start, 0)

    def last_copy(q):
        target = jnp.where(zone > 0, zone - 1, 0) * side
        return remote(last.at[part(q)], solved.at[zone, part(q)], s_last.at[q], s_recv.at[zone, q], col=target)

    def solve_last():
        high, low = split(work[...])
        for q in range(PARTS):
            value = solve(up_hi, up_lo, high, low, q)
            work[part(q)] = value
            last[part(q)] = value.astype(BF16)

            @pl.when(zone > 0)
            def _():
                last_copy(q).start()

    pl.when(jnp.logical_and(owner, zone > 0))(solve_last)
    first_products()
    lax.fori_loop(0, n_swap, second, 0)
    lax.fori_loop(0, n_extra, extra_hand_on, 0)
    pl.when(jnp.logical_and(owner, zone == 0))(solve_last)
    lax.fori_loop(0, n_extra, extra_product, 0)
    lax.fori_loop(0, n_swap, third, 0)

    @pl.when(owner)
    def _():
        out_ref[pl.ds(0, block)] = rhs_ref[...] - work[...]

    lax.fori_loop(0, n_swap, finish, 0)
    lax.fori_loop(0, n_extra, extra_finish, 0)

    @pl.when(sends_panel)
    def _():
        for d in range(chips):
            panel_copy(d).wait_send()

    for t in range(steps):
        j = slot(t)

        @pl.when(jnp.logical_and(owner, t != zone))
        def _():
            for p in range(pieces):
                source = j * pieces + p

                @pl.when(jnp.logical_and(source != row, source % 2 == core))
                def _():
                    forward_piece(source).wait_send()

        @pl.when(jnp.logical_and(owner, chain_sends(t)))
        def _():
            for q in range(PARTS):
                chain_copy(t, j, q).wait_send()

        @pl.when(owner)
        def _():
            for d in range(1, side):
                for q in range(PARTS):
                    side_copy(t, j, d, q).wait_send()

        for q in range(PARTS):
            @pl.when(j * pieces + q // per != row)
            def _():
                row_copy(t, j, q).wait_send()

    @pl.when(jnp.logical_and(owner, zone > 0))
    def _():
        for q in range(PARTS):
            last_copy(q).wait_send()


def body(rhs, factors, diag_inv):
    n_row, n_col = lax.axis_size("row"), lax.axis_size("col")
    rows_dev, width = rhs.shape
    cols = factors.shape[1]
    steps, block = diag_inv.shape[:2]
    pieces, chips, side = block // cols, n_row // 2, n_col // steps
    step_rows = rows_dev // CHUNKS
    dma = pltpu.SemaphoreType.DMA
    vmem = pl.BlockSpec(memory_space=pltpu.VMEM)
    taken = pl.pallas_call(
        functools.partial(kernel, n_row, n_col, steps, block),
        out_shape=jax.ShapeDtypeStruct(rhs.shape, F32),
        in_specs=[pl.BlockSpec(memory_space=pl.ANY)] * 3,
        out_specs=vmem,
        scratch_shapes=[
            pltpu.VMEM((block, width), F32),
            pltpu.VMEM(factors.shape, BF16),
            pltpu.VMEM((GATHER, n_row, step_rows, cols), BF16),
            pltpu.VMEM((block, block), F32),
            pltpu.VMEM((block, block), BF16),
            pltpu.VMEM((block, block), BF16),
            pltpu.VMEM((block, block), BF16),
            pltpu.VMEM((block, block), BF16),
            pltpu.VMEM((n_row, block, cols), BF16),
            pltpu.VMEM((steps, block, width), BF16),
            pltpu.VMEM((block, width), BF16),
            pltpu.VMEM((block, width), F32),
            pltpu.VMEM((2, cols, chips * width), BF16),
            pltpu.VMEM((CHUNKS, step_rows, chips * width), BF16),
            pltpu.VMEM((CHUNKS, step_rows, chips * width), BF16),
            pltpu.VMEM((CHUNKS, step_rows, chips * width), F32),
            pltpu.VMEM((CHUNKS, chips - 1, step_rows, width), BF16),
            pltpu.VMEM((CHUNKS, chips - 1, step_rows, width), BF16),
            dma, dma((chips,)), dma((n_row,)), dma((chips,)),
            dma((steps, PARTS)), dma((steps, side, PARTS)), dma((steps, PARTS)), dma((steps, PARTS)), dma((PARTS,)),
            dma((PARTS // pieces,)), dma((n_row, PARTS // pieces)),
            dma((CHUNKS,)), dma((CHUNKS,)), dma((CHUNKS, chips - 1)), dma((CHUNKS, chips - 1)),
            dma((GATHER, chips)), dma((GATHER, n_row)), dma((GATHER, chips)), dma((4,)),
        ],
        compiler_params=pltpu.CompilerParams(
            collective_id=0, has_side_effects=True, vmem_limit_bytes=60 * 1024 * 1024
        ),
    )(rhs, factors, diag_inv)
    return rhs - taken


def solution(mesh):
    placed = (P("col", "row"), P("col", "row"), P())
    return jax.shard_map(
        body, mesh=mesh, in_specs=placed, out_specs=P("col", "row"), check_vma=False
    )
```

profile of v0, /device:TPU:0, one launch (start us, length us, event | category | flops | bytes accessed | tf_op | source)
XLA Modules:
  0.0 72.9 jit_solution(5406840195497656402)
XLA Ops:
  0.0 0.0 copy-start
  0.0 69.8 %shard_map.37 = f32[4096,128]{1,0:T(8,128)} custom-call(f32[4096,128]{1,0:T(8,128)} %rhs_hbm.1, bf16[4096,512]{1,0:T(8,128)(2,1)} %factors_hbm.1, f32[4,512,512]{2,1,0:T(8,128)} %diag_ref.1), custom_call_target="tpu_custom_call" | custom-call | tf_op jit(solution)/shard_map/pallas_call | solution.py:410
  69.8 0.0 copy-done
  69.8 3.1 %sub.3 = f32[4096,128]{1,0:T(8,128)} subtract(f32[4096,128]{1,0:T(8,128)S(1)} %copy-done, f32[4096,128]{1,0:T(8,128)} %shard_map.37) | non-fusion elementwise | flops 524288 | bytes 6291456 | tf_op jit(solution)/shard_map/sub | solution.py:444
Async XLA Ops:
  0.0 69.8 %copy-start = (f32[4096,128]{1,0:T(8,128)S(1)}, f32[4096,128]{1,0:T(8,128)}, u32[]{:S(2)}) copy-start(f32[4096,128]{1,0:T(8,128)} %rhs_hbm.1) | copy-start | bytes 6291460
where the time goes:
time: 73.1 us; the launch traced here: 72.9 us
  Pallas kernels  69.8 us (95%)
  other arithmetic  3.12 us (4%)
    pallas_call x1, Pallas kernels, body(): pl.pallas_call(functools.partial(kernel, n_row, n_col, steps, block), out...  69.8 us
    sub x1, other arithmetic, body(): return rhs - taken  3.12 us

commit v1 on v0

v1 whole, which is shorter than its diff:
```python
import functools

import jax
import jax.numpy as jnp
from jax import lax
from jax.experimental import pallas as pl
from jax.experimental.pallas import tpu as pltpu
from jax.sharding import PartitionSpec as P

MESH = pl.DeviceIdType.MESH
F32 = jnp.float32
BF16 = jnp.bfloat16
CHUNKS = 8
SUBS = 2
CUTS = 2
GATHER = 3


def remote(src, dst, send_sem, recv_sem, **device):
    return pltpu.make_async_remote_copy(
        src_ref=src,
        dst_ref=dst,
        send_sem=send_sem,
        recv_sem=recv_sem,
        device_id=device,
        device_id_type=MESH,
    )


def dot(a, b):
    return jnp.dot(a, b, preferred_element_type=F32)


def dot_t(a, b):
    return lax.dot_general(a, b, (((1,), (1,)), ((), ())), preferred_element_type=F32)


def split(value):
    high = value.astype(BF16)
    return high, (value - high.astype(F32)).astype(BF16)


def kernel(
    n_row, n_col, steps, block,
    rhs_hbm, factors_hbm, diag_ref, out_ref,
    rhs_ref, factors_ref, extra,
    diag, low_hi, low_lo, up_hi, up_lo, panel, solved, last, work, state, gathered,
    send1, recv1, own1, send2, recv2,
    diag_sem, f_send, f_far, f_recv, f_fwd, s_chain, s_side, s_row, s_recv, s_last, g_local, g_recv,
    one_send, one_recv, two_send, two_recv, x_send, x_recv, x_fwd, load_sem,
):
    rows_dev, width = rhs_hbm.shape
    cols = factors_ref.shape[1]
    pieces = block // cols
    chips = n_row // 2
    side = n_col // steps
    row = lax.axis_index("row")
    col = lax.axis_index("col")
    chip, core = row // 2, row % 2
    sibling = chip * 2 + 1 - core
    zone, lane = col // side, col % side
    owner = lane == 0
    base = zone * side

    diag_copy = pltpu.make_async_copy(diag_ref.at[zone], diag, diag_sem)
    rhs_copy = pltpu.make_async_copy(rhs_hbm.at[pl.ds(0, block)], rhs_ref, load_sem.at[0])
    factors_copy = pltpu.make_async_copy(factors_hbm, factors_ref, load_sem.at[1])
    work_copy = pltpu.make_async_copy(rhs_hbm.at[pl.ds(0, block)], work, load_sem.at[2])
    panel_own = pltpu.make_async_copy(factors_hbm.at[pl.ds(0, block)], panel.at[row], load_sem.at[3])
    diag_copy.start()
    work_copy.start()
    panel_own.start()
    factors_copy.start()
    rhs_copy.start()

    barrier = pltpu.get_barrier_semaphore()
    for d in range(1, n_row):
        pl.semaphore_signal(barrier, inc=1, device_id={"row": (row + d) % n_row}, device_id_type=MESH)

    def greet(other):
        pl.semaphore_signal(barrier, inc=1, device_id={"col": other}, device_id_type=MESH)

    @pl.when(owner)
    def _():
        for d in range(1, side):
            greet(base + d)

    pl.when(jnp.logical_and(owner, zone > 0))(lambda: greet(base - side))
    pl.when(jnp.logical_and(owner, zone < steps - 1))(lambda: greet(base + side))
    pl.when(jnp.logical_not(owner))(lambda: greet(base))
    ends = jnp.where(zone > 0, 1, 0) + jnp.where(zone < steps - 1, 1, 0)
    pl.semaphore_wait(barrier, n_row - 1 + jnp.where(owner, ends + side - 1, 1))

    far = [((chip + d) % chips) * 2 + core for d in range(1, chips)]
    sends_panel = jnp.logical_and(owner, row // pieces != zone)
    half = block // 2
    cut_rows = half // CUTS
    pair = chip * 2
    later = pair // pieces > zone
    leading = jnp.where(later, pair + 1, pair)
    trailing = jnp.where(later, pair, pair + 1)

    def cut(h, c):
        return pl.ds(pl.multiple_of(h * half + c * cut_rows, cut_rows), cut_rows)

    def needed(source):
        return jnp.logical_and(owner, source // pieces != zone)

    def near_copy(h, c):
        rows = cut(h, c)
        return remote(factors_hbm.at[rows], panel.at[row, rows], f_send.at[h, c], f_recv.at[row, h, c], row=sibling)

    def far_copy(source, d, c):
        piece = panel.at[source, cut(core, c)]
        return remote(piece, piece, f_far.at[source % 2, d - 1, c], f_recv.at[source, core, c], row=far[d - 1])

    def relay_copy(source, h, c):
        piece = panel.at[source, cut(h, c)]
        return remote(piece, piece, f_fwd.at[source, c], f_recv.at[source, h, c], row=sibling)

    @pl.when(sends_panel)
    def _():
        for h in (1 - core, core):
            for c in range(CUTS):
                near_copy(h, c).start()

    def far_sends(source):
        @pl.when(needed(source))
        def _():
            @pl.when(source != row)
            def _():
                for c in range(CUTS):
                    relay_copy(source, core, c).wait_recv()

            for d in range(1, chips):
                for c in range(CUTS):
                    far_copy(source, d, c).start()

    panel_own.wait()
    pl.when(leading == row)(lambda: far_sends(leading))

    step_rows = rows_dev // CHUNKS
    n_extra = jnp.maximum(GATHER - (zone + 1) // 2 - jnp.where(owner, 1, 0), 0)

    def span(m):
        return pl.ds(pl.multiple_of(m * step_rows, step_rows), step_rows)

    def extra_copy(g, d):
        return remote(
            factors_hbm.at[span(CHUNKS - 1 - g)], extra.at[g, row], x_send.at[g, d], x_recv.at[g, row],
            row=far[d - 1] if d else sibling,
        )

    def extra_forward(g, source):
        return remote(extra.at[g, source], extra.at[g, source], x_fwd.at[g, source // 2], x_recv.at[g, source], row=sibling)

    def extra_start(g, carry):
        for d in range(chips):
            extra_copy(g, d).start()
        return carry

    waits = jnp.logical_and(owner, zone > 0)
    lax.fori_loop(0, jnp.where(owner, 0, n_extra), extra_start, 0)
    diag_copy.wait()
    work_copy.wait()

    @pl.when(owner)
    def _():
        down = lax.broadcasted_iota(jnp.int32, (block, block), 0)
        across = lax.broadcasted_iota(jnp.int32, (block, block), 1)
        matrix = diag[...]
        low_hi[...], low_lo[...] = split(jnp.where(down > across, matrix, 0.0))
        up_hi[...], up_lo[...] = split(jnp.where(down <= across, matrix, 0.0))
        state[...] = work[...].T

    sub = width // SUBS

    def batch(s, start=0):
        return pl.ds(pl.multiple_of(start + s * sub, sub), sub)

    def stacked(value):
        high, low = split(value)
        return high, jnp.concatenate([high, low])

    def folded(both, more):
        return both[:sub] + (both[sub:] + more)

    def solve_low(value):
        high, both = stacked(value)
        top = folded(dot_t(both[:, :half], low_hi[:half, :half]), dot_t(high[:, :half], low_lo[:half, :half]))
        return jnp.concatenate([top, folded(dot_t(both, low_hi[half:]), dot_t(high, low_lo[half:]))], axis=1)

    def solve_up(value):
        high, both = stacked(value)
        end = folded(dot_t(both[:, half:], up_hi[half:, half:]), dot_t(high[:, half:], up_lo[half:, half:]))
        return jnp.concatenate([folded(dot_t(both, up_hi[:half]), dot_t(high, up_lo[:half])), end], axis=1)

    def slot(t):
        return jnp.where(t <= zone, t, steps + zone - t)

    def is_far(source):
        return jnp.logical_and(owner, source // 2 != chip)

    def relay_panel(j):
        for p in range(pieces):
            source = j * pieces + p

            @pl.when(is_far(source))
            def _():
                for c in range(CUTS):
                    relay_copy(source, core, c).wait_recv()
                    relay_copy(source, core, c).start()

    def relay_back():
        def one(i, carry):
            relay_panel(steps - 1 - i)
            return carry

        lax.fori_loop(0, steps - 1 - zone, one, 0)

    def arrive_panel(j):
        for p in range(pieces):
            source = j * pieces + p

            @pl.when(source != row)
            def _():
                for c in range(CUTS):
                    relay_copy(source, 1 - core, c).wait_recv()

    def chain_copy(t, j, s):
        target = jnp.where(t <= zone, zone + 1, zone - 1)
        piece = solved.at[j, batch(s)]
        return remote(piece, piece, s_chain.at[t, s], s_recv.at[j, s], col=target * side)

    def chain_sends(t):
        return jnp.where(t <= zone, zone < steps - 1, zone > 0)

    def side_copy(t, j, d, s):
        piece = solved.at[j, batch(s)]
        return remote(piece, piece, s_side.at[t, d, s], s_recv.at[j, s], col=base + d)

    def row_copy(t, j, s, p):
        return remote(
            solved.at[j, batch(s), pl.ds(p * cols, cols)], gathered.at[core, batch(s, chip * width)],
            s_row.at[t, s, p], g_recv.at[row, s], row=j * pieces + p,
        )

    def local_copy(j, s, p):
        return pltpu.make_async_copy(
            solved.at[j, batch(s), pl.ds(p * cols, cols)], gathered.at[core, batch(s, chip * width)], g_local.at[s]
        )

    def pass_on(t, j, s):
        pl.when(jnp.logical_and(owner, chain_sends(t)))(lambda: chain_copy(t, j, s).start())

        @pl.when(owner)
        def _():
            for d in range(1, side):
                side_copy(t, j, d, s).start()

        for p in range(pieces):
            pl.when(j * pieces + p != row)(lambda: row_copy(t, j, s, p).start())
            pl.when(j * pieces + p == row)(lambda: local_copy(j, s, p).start())

    def update(j, s):
        total = state[batch(s)]
        for p in range(pieces):
            total = total - dot_t(solved[j, batch(s), pl.ds(p * cols, cols)], panel[j * pieces + p])
        state[batch(s)] = total

    def solve_first(s):
        value = state[batch(s)]
        value = value + solve_low(value)
        state[batch(s)] = value
        solved[zone, batch(s)] = value.astype(BF16)
        pass_on(zone, zone, s)

    def last_copy(s):
        target = jnp.where(zone > 0, zone - 1, 0) * side
        return remote(last.at[batch(s)], solved.at[zone, batch(s)], s_last.at[s], s_recv.at[zone, s], col=target)

    def solve_last(s):
        value = solve_up(state[batch(s)])
        state[batch(s)] = value
        last[batch(s)] = value.astype(BF16)
        pl.when(zone > 0)(lambda: last_copy(s).start())

    def one_copy(m):
        return remote(send1.at[m], recv1.at[m], one_send.at[m], one_recv.at[m], row=sibling)

    def two_copy(m, d):
        return remote(send2.at[m, d - 1], recv2.at[m, d - 1], two_send.at[m, d - 1], two_recv.at[m, d - 1], row=far[d - 1])

    def first(m, carry):
        send1[m] = dot_t(factors_ref[span(m)], gathered[1 - core]).astype(BF16)
        one_copy(m).start()
        return carry

    def second(m, carry):
        @pl.when(m + 1 < n_swap)
        def _():
            first(m + 1, 0)

        own1[m] = dot_t(factors_ref[span(m)], gathered[core])
        one_copy(m).wait_recv()
        for d in range(1, chips):
            there = pl.ds(pl.multiple_of(((chip + d) % chips) * width, width), width)
            send2[m, d - 1] = (own1[m, :, there] + recv1[m, :, there].astype(F32)).astype(BF16)
            two_copy(m, d).start()
        return carry

    def third(m, carry):
        here = pl.ds(pl.multiple_of(chip * width, width), width)
        total = own1[m, :, here] + recv1[m, :, here].astype(F32)
        for d in range(1, chips):
            two_copy(m, d).wait_recv()
            total = total + recv2[m, d - 1].astype(F32)
        out_ref[span(m)] = total
        return carry

    def finish(m, carry):
        one_copy(m).wait_send()
        for d in range(1, chips):
            two_copy(m, d).wait_send()
        return carry

    n_swap = CHUNKS - n_extra

    def extra_hand_on(g, carry):
        for d in range(1, chips):
            extra_forward(g, far[d - 1]).wait_recv()
            extra_forward(g, far[d - 1]).start()
        return carry

    def extra_product(g, carry):
        rows = span(CHUNKS - 1 - g)
        total = jnp.zeros((step_rows, width), F32)
        for d in range(n_row):
            source = (row + d) % n_row
            part_of = solved[source // pieces, :, pl.ds(pl.multiple_of((source % pieces) * cols, cols), cols)]
            if d == 0:
                total = total + dot_t(factors_ref[rows], part_of)
            else:
                @pl.when(source % 2 != core)
                def _():
                    extra_forward(g, source).wait_recv()

                total = total + dot_t(extra[g, source], part_of)
        out_ref[rows] = total
        return carry

    def extra_finish(g, carry):
        for d in range(chips):
            extra_copy(g, d).wait_send()
        for d in range(1, chips):
            extra_forward(g, far[d - 1]).wait_send()
        return carry

    def first_products():
        factors_copy.wait()
        rhs_copy.wait()

        def arrive(s, carry):
            local_copy(0, s, 0).wait()
            for d in range(1, n_row):
                source = (row + d) % n_row
                piece = gathered.at[source % 2, batch(s, (source // 2) * width)]
                remote(piece, piece, g_local.at[s], g_recv.at[source, s], row=source).wait_recv()
            return carry

        lax.fori_loop(0, SUBS, arrive, 0)
        first(0, 0)

    def batches(what):
        def one(s, carry):
            what(s)
            return carry

        lax.fori_loop(0, SUBS, one, 0)

    @pl.when(owner)
    def _():
        pl.when(zone == 0)(lambda: batches(solve_first))
        pl.when(leading != row)(lambda: far_sends(leading))
        far_sends(trailing)
        lax.fori_loop(0, jnp.where(zone == 0, n_extra, 0), extra_start, 0)
        pl.when(zone == 0)(relay_back)

        def hop(i, carry):
            t = jnp.where(i < zone, i, i + 1)
            j = slot(t)

            late = jnp.logical_and(is_far(j * pieces), i < zone)

            def take(s):
                chain_copy(t, j, s).wait_recv()
                pass_on(t, j, s)

            @pl.when(late)
            def _():
                batches(take)
                relay_panel(j)

            def one(s):
                pl.when(jnp.logical_not(late))(lambda: take(s))
                pl.when(s == 0)(lambda: arrive_panel(j))
                update(j, s)
                pl.when(i + 1 == zone)(lambda: solve_first(s))
                pl.when(jnp.logical_and(i == steps - 2, zone > 0))(lambda: solve_last(s))

            batches(one)
            lax.fori_loop(0, jnp.where(jnp.logical_and(waits, i == 0), n_extra, 0), extra_start, 0)
            pl.when(i + 1 == zone)(relay_back)
            return carry

        lax.fori_loop(0, steps - 1, hop, 0)

    @pl.when(jnp.logical_not(owner))
    def _():
        def hop(t, carry):
            j = slot(t)

            def one(s):
                chain_copy(t, j, s).wait_recv()
                pass_on(t, j, s)

            batches(one)
            return carry

        lax.fori_loop(0, steps, hop, 0)

    first_products()
    lax.fori_loop(0, n_swap, second, 0)
    lax.fori_loop(0, n_extra, extra_hand_on, 0)
    pl.when(jnp.logical_and(owner, zone == 0))(lambda: batches(solve_last))
    lax.fori_loop(0, n_extra, extra_product, 0)
    lax.fori_loop(0, n_swap, third, 0)

    @pl.when(owner)
    def _():
        out_ref[pl.ds(0, block)] = rhs_ref[...] - state[...].T

    lax.fori_loop(0, n_swap, finish, 0)
    lax.fori_loop(0, n_extra, extra_finish, 0)

    @pl.when(sends_panel)
    def _():
        for h in range(2):
            for c in range(CUTS):
                near_copy(h, c).wait_send()

    for source in (pair, pair + 1):
        @pl.when(needed(source))
        def _():
            for d in range(1, chips):
                for c in range(CUTS):
                    far_copy(source, d, c).wait_send()

    def drain(t, carry):
        j = slot(t)

        for p in range(pieces):
            source = j * pieces + p

            @pl.when(jnp.logical_and(is_far(source), t != zone))
            def _():
                for c in range(CUTS):
                    relay_copy(source, core, c).wait_send()

        def one(s):
            pl.when(jnp.logical_and(owner, chain_sends(t)))(lambda: chain_copy(t, j, s).wait_send())

            @pl.when(owner)
            def _():
                for d in range(1, side):
                    side_copy(t, j, d, s).wait_send()

            for p in range(pieces):
                pl.when(j * pieces + p != row)(lambda: row_copy(t, j, s, p).wait_send())

        batches(one)
        return carry

    lax.fori_loop(0, steps, drain, 0)

    @pl.when(jnp.logical_and(owner, zone > 0))
    def _():
        batches(lambda s: last_copy(s).wait_send())


def body(rhs, factors, diag_inv):
    n_row, n_col = lax.axis_size("row"), lax.axis_size("col")
    rows_dev, width = rhs.shape
    cols = factors.shape[1]
    steps, block = diag_inv.shape[:2]
    pieces, chips, side = block // cols, n_row // 2, n_col // steps
    step_rows = rows_dev // CHUNKS
    dma = pltpu.SemaphoreType.DMA
    vmem = pl.BlockSpec(memory_space=pltpu.VMEM)
    taken = pl.pallas_call(
        functools.partial(kernel, n_row, n_col, steps, block),
        out_shape=jax.ShapeDtypeStruct(rhs.shape, F32),
        in_specs=[pl.BlockSpec(memory_space=pl.ANY)] * 3,
        out_specs=vmem,
        scratch_shapes=[
            pltpu.VMEM((block, width), F32),
            pltpu.VMEM(factors.shape, BF16),
            pltpu.VMEM((GATHER, n_row, step_rows, cols), BF16),
            pltpu.VMEM((block, block), F32),
            pltpu.VMEM((block, block), BF16),
            pltpu.VMEM((block, block), BF16),
            pltpu.VMEM((block, block), BF16),
            pltpu.VMEM((block, block), BF16),
            pltpu.VMEM((n_row, block, cols), BF16),
            pltpu.VMEM((steps, width, block), BF16),
            pltpu.VMEM((width, block), BF16),
            pltpu.VMEM((block, width), F32),
            pltpu.VMEM((width, block), F32),
            pltpu.VMEM((2, chips * width, cols), BF16),
            pltpu.VMEM((CHUNKS, step_rows, chips * width), BF16),
            pltpu.VMEM((CHUNKS, step_rows, chips * width), BF16),
            pltpu.VMEM((CHUNKS, step_rows, chips * width), F32),
            pltpu.VMEM((CHUNKS, chips - 1, step_rows, width), BF16),
            pltpu.VMEM((CHUNKS, chips - 1, step_rows, width), BF16),
            dma, dma((2, CUTS)), dma((2, chips - 1, CUTS)), dma((n_row, 2, CUTS)), dma((n_row, CUTS)),
            dma((steps, SUBS)), dma((steps, side, SUBS)), dma((steps, SUBS, pieces)), dma((steps, SUBS)), dma((SUBS,)),
            dma((SUBS,)), dma((n_row, SUBS)),
            dma((CHUNKS,)), dma((CHUNKS,)), dma((CHUNKS, chips - 1)), dma((CHUNKS, chips - 1)),
            dma((GATHER, chips)), dma((GATHER, n_row)), dma((GATHER, chips)), dma((4,)),
        ],
        compiler_params=pltpu.CompilerParams(
            collective_id=0, has_side_effects=True, vmem_limit_bytes=50 * 1024 * 1024
        ),
    )(rhs, factors, diag_inv)
    return rhs - taken


def solution(mesh):
    placed = (P("col", "row"), P("col", "row"), P())
    return jax.shard_map(
        body, mesh=mesh, in_specs=placed, out_specs=P("col", "row"), check_vma=False
    )
```

time: 73.1 us -> 67 us (0.917)
  Pallas kernels: 69.8 us -> 65.3 us
  other arithmetic: 3.12 us -> 1.53 us
    pallas_call x1, Pallas kernels: 69.8 us -> 65.3 us  [body(): pl.pallas_call(functools.partial(kernel, n_row, n_col, steps, block), out...]
    sub x1, other arithmetic: 3.12 us -> 1.53 us  [body(): return rhs - taken]
where the time goes in v1:
time: 67 us; the launch traced here: 66.9 us
  Pallas kernels  65.3 us (97%)
  other arithmetic  1.53 us (2%)
    pallas_call x1, Pallas kernels, body(): pl.pallas_call(functools.partial(kernel, n_row, n_col, steps, block), out...  65.3 us
    sub x1, other arithmetic, body(): return rhs - taken  1.53 us

profile of v1, /device:TPU:0, one launch (start us, length us, event | category | flops | bytes accessed | tf_op | source)
XLA Modules:
  0.0 66.9 jit_solution(2234278713439396023)
XLA Ops:
  0.0 0.0 copy-start
  0.0 65.3 %shard_map.37 = f32[4096,128]{1,0:T(8,128)S(1)} custom-call(f32[4096,128]{1,0:T(8,128)} %rhs_hbm.1, bf16[4096,512]{1,0:T(8,128)(2,1)} %factors_hbm.1, f32[4,512,512]{2,1,0:T(8,128)} %diag_ref.1), custom_call_target="tpu_custom_call" | custom-call | tf_op jit(solution)/shard_map/pallas_call | solution.py:500
  65.3 0.0 copy-done
  65.3 1.5 %sub.3 = f32[4096,128]{1,0:T(8,128)} subtract(f32[4096,128]{1,0:T(8,128)S(1)} %copy-done, f32[4096,128]{1,0:T(8,128)S(1)} %shard_map.37) | non-fusion elementwise | flops 524288 | bytes 6291456 | tf_op jit(solution)/shard_map/sub | solution.py:535
Async XLA Ops:
  0.0 65.3 %copy-start = (f32[4096,128]{1,0:T(8,128)S(1)}, f32[4096,128]{1,0:T(8,128)}, u32[]{:S(2)}) copy-start(f32[4096,128]{1,0:T(8,128)} %rhs_hbm.1) | copy-start | bytes 6291460

commit v2 on v1

--- a/solution.py
+++ b/solution.py
@@ -13,7 +13,9 @@
 CHUNKS = 8
 SUBS = 2
 CUTS = 2
-GATHER = 3
+GATHER = 4
+NEAR0, FAR0, NEAR1, FAR1, REST1 = 2, 3, 4, 4, 2
+HEAD0, HEAD1 = 2, 4
 
 
 def remote(src, dst, send_sem, recv_sem, **device):
@@ -43,11 +45,11 @@
 def kernel(
     n_row, n_col, steps, block,
     rhs_hbm, factors_hbm, diag_ref, out_ref,
-    rhs_ref, factors_ref, extra,
+    rhs_ref, factors_ref, extra, taken,
     diag, low_hi, low_lo, up_hi, up_lo, panel, solved, last, work, state, gathered,
     send1, recv1, own1, send2, recv2,
-    diag_sem, f_send, f_far, f_recv, f_fwd, s_chain, s_side, s_row, s_recv, s_last, g_local, g_recv,
-    one_send, one_recv, two_send, two_recv, x_send, x_recv, x_fwd, load_sem,
+    diag_sem, f_send, f_far, f_recv, f_fwd, s_chain, s_side, s_row, s_lend, s_help, s_hint, s_recv, l_recv, s_last, g_local, g_recv,
+    one_send, one_recv, two_send, two_recv, x_send, x_recv, x_fwd, load_sem, out_sem,
 ):
     rows_dev, width = rhs_hbm.shape
     cols = factors_ref.shape[1]
@@ -60,6 +62,7 @@
     sibling = chip * 2 + 1 - core
     zone, lane = col // side, col % side
     owner = lane == 0
+    helper = lane == 1
     base = zone * side
 
     diag_copy = pltpu.make_async_copy(diag_ref.at[zone], diag, diag_sem)
@@ -67,11 +70,12 @@
     factors_copy = pltpu.make_async_copy(factors_hbm, factors_ref, load_sem.at[1])
     work_copy = pltpu.make_async_copy(rhs_hbm.at[pl.ds(0, block)], work, load_sem.at[2])
     panel_own = pltpu.make_async_copy(factors_hbm.at[pl.ds(0, block)], panel.at[row], load_sem.at[3])
-    diag_copy.start()
-    work_copy.start()
-    panel_own.start()
-    factors_copy.start()
-    rhs_copy.start()
+    @pl.when(owner)
+    def _():
+        diag_copy.start()
+        work_copy.start()
+        panel_own.start()
+
 
     barrier = pltpu.get_barrier_semaphore()
     for d in range(1, n_row):
@@ -88,8 +92,10 @@
     pl.when(jnp.logical_and(owner, zone > 0))(lambda: greet(base - side))
     pl.when(jnp.logical_and(owner, zone < steps - 1))(lambda: greet(base + side))
     pl.when(jnp.logical_not(owner))(lambda: greet(base))
+    for z in range(1, steps - 2):
+        pl.when(jnp.logical_and(owner, zone > z + 1))(lambda: greet(z * side + 1))
+    beyond = jnp.where(jnp.logical_and(zone > 0, zone < steps - 2), steps - 2 - zone, 0)
     ends = jnp.where(zone > 0, 1, 0) + jnp.where(zone < steps - 1, 1, 0)
-    pl.semaphore_wait(barrier, n_row - 1 + jnp.where(owner, ends + side - 1, 1))
 
     far = [((chip + d) % chips) * 2 + core for d in range(1, chips)]
     sends_panel = jnp.logical_and(owner, row // pieces != zone)
@@ -118,12 +124,6 @@
         piece = panel.at[source, cut(h, c)]
         return remote(piece, piece, f_fwd.at[source, c], f_recv.at[source, h, c], row=sibling)
 
-    @pl.when(sends_panel)
-    def _():
-        for h in (1 - core, core):
-            for c in range(CUTS):
-                near_copy(h, c).start()
-
     def far_sends(source):
         @pl.when(needed(source))
         def _():
@@ -136,11 +136,16 @@
                 for c in range(CUTS):
                     far_copy(source, d, c).start()
 
-    panel_own.wait()
-    pl.when(leading == row)(lambda: far_sends(leading))
 
     step_rows = rows_dev // CHUNKS
-    n_extra = jnp.maximum(GATHER - (zone + 1) // 2 - jnp.where(owner, 1, 0), 0)
+
+    def want(c):
+        first_zone = jnp.where(owner, jnp.where(c * 2 < chips, NEAR0, FAR0), jnp.where(c * 2 < chips, NEAR1, FAR1))
+        return jnp.where(zone == 0, first_zone, jnp.where(owner, jnp.where(zone < steps - 1, 1, 0), REST1))
+
+    n_extra = want(chip)
+    wants = [want((chip + d) % chips) for d in range(chips)]
+    head = jnp.where(owner, HEAD0, HEAD1)
 
     def span(m):
         return pl.ds(pl.multiple_of(m * step_rows, step_rows), step_rows)
@@ -156,23 +161,10 @@
 
     def extra_start(g, carry):
         for d in range(chips):
-            extra_copy(g, d).start()
+            pl.when(g < wants[d])(lambda: extra_copy(g, d).start())
         return carry
 
     waits = jnp.logical_and(owner, zone > 0)
-    lax.fori_loop(0, jnp.where(owner, 0, n_extra), extra_start, 0)
-    diag_copy.wait()
-    work_copy.wait()
-
-    @pl.when(owner)
-    def _():
-        down = lax.broadcasted_iota(jnp.int32, (block, block), 0)
-        across = lax.broadcasted_iota(jnp.int32, (block, block), 1)
-        matrix = diag[...]
-        low_hi[...], low_lo[...] = split(jnp.where(down > across, matrix, 0.0))
-        up_hi[...], up_lo[...] = split(jnp.where(down <= across, matrix, 0.0))
-        state[...] = work[...].T
-
     sub = width // SUBS
 
     def batch(s, start=0):
@@ -227,17 +219,60 @@
                 for c in range(CUTS):
                     relay_copy(source, 1 - core, c).wait_recv()
 
-    def chain_copy(t, j, s):
-        target = jnp.where(t <= zone, zone + 1, zone - 1)
+    def chain_copy(t, s):
+        piece = solved.at[t, batch(s)]
+        k = jnp.where(t == 0, 0, 1)
+        return remote(
+            piece, piece, s_chain.at[k, s], s_recv.at[t, s], col=jnp.minimum(zone + 1, steps - 1) * side
+        )
+
+    def chains(t):
+        return jnp.logical_and(owner, jnp.logical_and((t == 0) | (t == zone), zone < steps - 1))
+
+    def arrival(j, s):
         piece = solved.at[j, batch(s)]
-        return remote(piece, piece, s_chain.at[t, s], s_recv.at[j, s], col=target * side)
-
-    def chain_sends(t):
-        return jnp.where(t <= zone, zone < steps - 1, zone > 0)
+        return remote(piece, piece, s_chain.at[0, s], s_recv.at[j, s], col=col)
+
+    def help_copy(z, s):
+        piece = solved.at[zone, batch(s)]
+        return remote(piece, piece, s_help.at[z, s], s_recv.at[zone, s], col=z * side)
+
+    def help_last(z, s):
+        return remote(last.at[batch(s)], solved.at[zone, batch(s)], s_help.at[z, s], s_recv.at[zone, s], col=z * side)
+
+    def hint_copy(d, s):
+        return remote(last.at[batch(s)], last.at[batch(s)], s_hint.at[d, s], l_recv.at[s], col=base + d)
+
+    def lane_last(s):
+        return remote(last.at[batch(s)], solved.at[zone, batch(s)], s_chain.at[0, s], s_recv.at[zone, s], col=lane)
+
+    def skip_last(s):
+        target = jnp.maximum(zone - 2, 0) * side
+        return remote(last.at[batch(s)], solved.at[zone, batch(s)], s_chain.at[2, s], s_recv.at[zone, s], col=target)
+
+    def forwards(what, s):
+        for z in range(2, steps):
+            pl.when(jnp.logical_and(helper, jnp.logical_and(z > zone + 1, zone > 0)))(
+                lambda: what(help_copy(z, s))
+            )
+
+    def backwards(what, s):
+        for z in reversed(range(steps - 3)):
+            pl.when(jnp.logical_and(helper, z < zone - 2))(lambda: what(help_last(z, s)))
+        what(lane_last(s))
+
+    def begin(copy):
+        copy.start()
+
+    def finished(copy):
+        copy.wait_send()
 
     def side_copy(t, j, d, s):
         piece = solved.at[j, batch(s)]
         return remote(piece, piece, s_side.at[t, d, s], s_recv.at[j, s], col=base + d)
+
+    def lends(t):
+        return jnp.logical_and(zone == 0, t < steps)
 
     def row_copy(t, j, s, p):
         return remote(
@@ -250,16 +285,46 @@
             solved.at[j, batch(s), pl.ds(p * cols, cols)], gathered.at[core, batch(s, chip * width)], g_local.at[s]
         )
 
+    def shares(t, j, s, what):
+        for p in range(pieces):
+            target = j * pieces + p
+            lent = jnp.logical_and(lends(t), target // 2 != chip)
+            sends = jnp.logical_and(target != row, jnp.logical_or(owner, jnp.logical_not(lent)))
+            pl.when(sends)(lambda: what(row_copy(t, j, s, p)))
+
+    my_turn = jnp.where(row // pieces == 0, 0, steps - row // pieces)
+    lender = jnp.logical_and(owner, lends(my_turn))
+
+    def lend_copy(d, k, s):
+        source = far[k // 2] // 2 * 2 + k % 2
+        piece = gathered.at[k % 2, batch(s, (source // 2) * width)]
+        return remote(piece, piece, s_lend.at[d, k, s], g_recv.at[source, s], col=base + d)
+
+    def lend(s):
+        for k in range(2 * (chips - 1)):
+            lend_copy(1, k, s).wait_recv()
+            for d in range(1, side):
+                lend_copy(d, k, s).start()
+
+    put_off = zone == steps - 1
+
+    def has_sides(j):
+        return jnp.logical_and(owner, jnp.logical_or(zone > 0, j < 2))
+
+    def sides(t, j, s):
+        for d in range(1, side):
+            side_copy(t, j, d, s).start()
+
     def pass_on(t, j, s):
-        pl.when(jnp.logical_and(owner, chain_sends(t)))(lambda: chain_copy(t, j, s).start())
-
-        @pl.when(owner)
+        pl.when(chains(t))(lambda: chain_copy(t, s).start())
+
+        @pl.when(jnp.logical_and(has_sides(j), jnp.logical_not(jnp.logical_and(put_off, t < zone))))
         def _():
-            for d in range(1, side):
-                side_copy(t, j, d, s).start()
-
+            sides(t, j, s)
+
+        pl.when(t == zone)(lambda: forwards(begin, s))
+        shares(t, j, s, begin)
         for p in range(pieces):
-            pl.when(j * pieces + p != row)(lambda: row_copy(t, j, s, p).start())
             pl.when(j * pieces + p == row)(lambda: local_copy(j, s, p).start())
 
     def update(j, s):
@@ -268,12 +333,13 @@
             total = total - dot_t(solved[j, batch(s), pl.ds(p * cols, cols)], panel[j * pieces + p])
         state[batch(s)] = total
 
-    def solve_first(s):
+    def solve_first(s, sends=True):
         value = state[batch(s)]
         value = value + solve_low(value)
         state[batch(s)] = value
         solved[zone, batch(s)] = value.astype(BF16)
-        pass_on(zone, zone, s)
+        if sends:
+            pass_on(zone, zone, s)
 
     def last_copy(s):
         target = jnp.where(zone > 0, zone - 1, 0) * side
@@ -285,6 +351,15 @@
         last[batch(s)] = value.astype(BF16)
         pl.when(zone > 0)(lambda: last_copy(s).start())
 
+        @pl.when(zone > 1)
+        def _():
+            for d in range(1, side):
+                hint_copy(d, s).start()
+
+
+    def out_copy(m):
+        return pltpu.make_async_copy(taken.at[span(m)], out_ref.at[span(m)], out_sem.at[m])
+
     def one_copy(m):
         return remote(send1.at[m], recv1.at[m], one_send.at[m], one_recv.at[m], row=sibling)
 
@@ -297,7 +372,7 @@
         return carry
 
     def second(m, carry):
-        @pl.when(m + 1 < n_swap)
+        @pl.when(m + 1 < n_made)
         def _():
             first(m + 1, 0)
 
@@ -305,8 +380,12 @@
         one_copy(m).wait_recv()
         for d in range(1, chips):
             there = pl.ds(pl.multiple_of(((chip + d) % chips) * width, width), width)
-            send2[m, d - 1] = (own1[m, :, there] + recv1[m, :, there].astype(F32)).astype(BF16)
-            two_copy(m, d).start()
+
+            @pl.when(m < CHUNKS - wants[d])
+            def _():
+                send2[m, d - 1] = (own1[m, :, there] + recv1[m, :, there].astype(F32)).astype(BF16)
+                two_copy(m, d).start()
+
         return carry
 
     def third(m, carry):
@@ -315,16 +394,22 @@
         for d in range(1, chips):
             two_copy(m, d).wait_recv()
             total = total + recv2[m, d - 1].astype(F32)
-        out_ref[span(m)] = total
+        taken[span(m)] = total
+        out_copy(m).start()
         return carry
 
     def finish(m, carry):
         one_copy(m).wait_send()
         for d in range(1, chips):
-            two_copy(m, d).wait_send()
+            pl.when(m < CHUNKS - wants[d])(lambda: two_copy(m, d).wait_send())
         return carry
 
     n_swap = CHUNKS - n_extra
+    fewest = wants[0]
+    for d in range(1, chips):
+        fewest = jnp.minimum(fewest, wants[d])
+    n_made = CHUNKS - fewest
+    start = jnp.where(owner, block // step_rows, 0)
 
     def extra_hand_on(g, carry):
         for d in range(1, chips):
@@ -346,14 +431,19 @@
                     extra_forward(g, source).wait_recv()
 
                 total = total + dot_t(extra[g, source], part_of)
-        out_ref[rows] = total
+        taken[rows] = total
+        out_copy(CHUNKS - 1 - g).start()
         return carry
 
     def extra_finish(g, carry):
         for d in range(chips):
-            extra_copy(g, d).wait_send()
-        for d in range(1, chips):
-            extra_forward(g, far[d - 1]).wait_send()
+            pl.when(g < wants[d])(lambda: extra_copy(g, d).wait_send())
+
+        @pl.when(g < n_extra)
+        def _():
+            for d in range(1, chips):
+                extra_forward(g, far[d - 1]).wait_send()
+
         return carry
 
     def first_products():
@@ -365,11 +455,13 @@
             for d in range(1, n_row):
                 source = (row + d) % n_row
                 piece = gathered.at[source % 2, batch(s, (source // 2) * width)]
-                remote(piece, piece, g_local.at[s], g_recv.at[source, s], row=source).wait_recv()
+                taken_on = jnp.logical_and(lender, source // 2 != chip)
+                arrived = remote(piece, piece, g_local.at[s], g_recv.at[source, s], row=source)
+                pl.when(jnp.logical_not(taken_on))(arrived.wait_recv)
             return carry
 
         lax.fori_loop(0, SUBS, arrive, 0)
-        first(0, 0)
+        first(start, 0)
 
     def batches(what):
         def one(s, carry):
@@ -378,12 +470,53 @@
 
         lax.fori_loop(0, SUBS, one, 0)
 
+    def prepare():
+        diag_copy.wait()
+        work_copy.wait()
+        down = lax.broadcasted_iota(jnp.int32, (block, block), 0)
+        across = lax.broadcasted_iota(jnp.int32, (block, block), 1)
+        matrix = diag[...]
+        low_hi[...], low_lo[...] = split(jnp.where(down > across, matrix, 0.0))
+        up_hi[...], up_lo[...] = split(jnp.where(down <= across, matrix, 0.0))
+        state[...] = work[...].T
+
+    def products():
+        first_products()
+        lax.fori_loop(start, n_made, second, 0)
+
+    final = slot(steps - 1) * pieces // 2
+    sooner = jnp.logical_and(jnp.logical_not(owner), jnp.logical_and(zone == 0, final != chip))
+    opens = jnp.logical_and(owner, zone == 0)
+
+    @pl.when(opens)
+    def _():
+        prepare()
+        batches(lambda s: solve_first(s, False))
+
+    pl.semaphore_wait(barrier, n_row - 1 + jnp.where(owner, ends + side - 1, 1 + jnp.where(helper, beyond, 0)))
+    @pl.when(sends_panel)
+    def _():
+        for h in (1 - core, core):
+            for c in range(CUTS):
+                near_copy(h, c).start()
+
     @pl.when(owner)
     def _():
-        pl.when(zone == 0)(lambda: batches(solve_first))
+        panel_own.wait()
+        pl.when(leading == row)(lambda: far_sends(leading))
+
+    pl.when(opens)(lambda: batches(lambda s: pass_on(zone, zone, s)))
+    lax.fori_loop(0, jnp.where(owner, 0, head), extra_start, 0)
+    pl.when(jnp.logical_and(owner, zone > 0))(prepare)
+    factors_copy.start()
+    rhs_copy.start()
+
+    @pl.when(owner)
+    def _():
+
         pl.when(leading != row)(lambda: far_sends(leading))
         far_sends(trailing)
-        lax.fori_loop(0, jnp.where(zone == 0, n_extra, 0), extra_start, 0)
+        lax.fori_loop(0, jnp.where(zone == 0, head, 0), extra_start, 0)
         pl.when(zone == 0)(relay_back)
 
         def hop(i, carry):
@@ -393,7 +526,7 @@
             late = jnp.logical_and(is_far(j * pieces), i < zone)
 
             def take(s):
-                chain_copy(t, j, s).wait_recv()
+                arrival(j, s).wait_recv()
                 pass_on(t, j, s)
 
             @pl.when(late)
@@ -409,39 +542,60 @@
                 pl.when(jnp.logical_and(i == steps - 2, zone > 0))(lambda: solve_last(s))
 
             batches(one)
-            lax.fori_loop(0, jnp.where(jnp.logical_and(waits, i == 0), n_extra, 0), extra_start, 0)
+            lax.fori_loop(0, jnp.where(jnp.logical_and(waits, i == 0), head, 0), extra_start, 0)
+            lax.fori_loop(head, jnp.where(i == 1, GATHER, head), extra_start, 0)
             pl.when(i + 1 == zone)(relay_back)
+            pl.when(jnp.logical_and(lender, i == jnp.maximum(my_turn - 1, 0)))(lambda: batches(lend))
             return carry
 
         lax.fori_loop(0, steps - 1, hop, 0)
 
+        pl.when(zone > 1)(lambda: batches(lambda s: skip_last(s).start()))
+
+        @pl.when(put_off)
+        def _():
+            for t in range(steps - 1):
+                batches(lambda s: sides(t, t, s))
+
     @pl.when(jnp.logical_not(owner))
     def _():
-        def hop(t, carry):
+        def hop(i, carry):
+            t = jnp.where(put_off, (i + steps - 1) % steps, i)
             j = slot(t)
 
             def one(s):
-                chain_copy(t, j, s).wait_recv()
+                arrival(j, s).wait_recv()
                 pass_on(t, j, s)
 
+                @pl.when(jnp.logical_and(t == steps - 1, zone > 1))
+                def _():
+                    hint_copy(1, s).wait_recv()
+                    backwards(begin, s)
+
             batches(one)
+            lax.fori_loop(head, jnp.where(i == 2, GATHER, head), extra_start, 0)
             return carry
 
-        lax.fori_loop(0, steps, hop, 0)
-
-    first_products()
-    lax.fori_loop(0, n_swap, second, 0)
+        def each(i, carry):
+            pl.when(jnp.logical_and(sooner, i == steps - 1))(products)
+            return hop(i, carry)
+
+        lax.fori_loop(0, steps, each, 0)
+
+    pl.when(jnp.logical_not(sooner))(products)
     lax.fori_loop(0, n_extra, extra_hand_on, 0)
     pl.when(jnp.logical_and(owner, zone == 0))(lambda: batches(solve_last))
     lax.fori_loop(0, n_extra, extra_product, 0)
-    lax.fori_loop(0, n_swap, third, 0)
 
     @pl.when(owner)
     def _():
-        out_ref[pl.ds(0, block)] = rhs_ref[...] - state[...].T
-
-    lax.fori_loop(0, n_swap, finish, 0)
-    lax.fori_loop(0, n_extra, extra_finish, 0)
+        taken[pl.ds(0, block)] = rhs_ref[...] - state[...].T
+        for m in range(block // step_rows):
+            out_copy(m).start()
+
+    lax.fori_loop(start, n_swap, third, 0)
+    lax.fori_loop(start, n_made, finish, 0)
+    lax.fori_loop(0, GATHER, extra_finish, 0)
 
     @pl.when(sends_panel)
     def _():
@@ -456,6 +610,10 @@
                 for c in range(CUTS):
                     far_copy(source, d, c).wait_send()
 
+    def written(m, carry):
+        out_copy(m).wait()
+        return carry
+
     def drain(t, carry):
         j = slot(t)
 
@@ -468,24 +626,42 @@
                     relay_copy(source, core, c).wait_send()
 
         def one(s):
-            pl.when(jnp.logical_and(owner, chain_sends(t)))(lambda: chain_copy(t, j, s).wait_send())
-
-            @pl.when(owner)
+            pl.when(chains(t))(lambda: chain_copy(t, s).wait_send())
+            pl.when(t == zone)(lambda: forwards(finished, s))
+
+            @pl.when(has_sides(j))
             def _():
                 for d in range(1, side):
                     side_copy(t, j, d, s).wait_send()
 
-            for p in range(pieces):
-                pl.when(j * pieces + p != row)(lambda: row_copy(t, j, s, p).wait_send())
+            shares(t, j, s, finished)
 
         batches(one)
         return carry
 
     lax.fori_loop(0, steps, drain, 0)
 
+    lax.fori_loop(0, CHUNKS, written, 0)
+
+    @pl.when(lender)
+    def _():
+        for d in range(1, side):
+            for k in range(2 * (chips - 1)):
+                batches(lambda s: lend_copy(d, k, s).wait_send())
+
     @pl.when(jnp.logical_and(owner, zone > 0))
     def _():
         batches(lambda s: last_copy(s).wait_send())
+
+    @pl.when(jnp.logical_and(owner, zone > 1))
+    def _():
+        batches(lambda s: skip_last(s).wait_send())
+        for d in range(1, side):
+            batches(lambda s: hint_copy(d, s).wait_send())
+
+    @pl.when(jnp.logical_and(jnp.logical_not(owner), zone > 1))
+    def _():
+        batches(lambda s: backwards(finished, s))
 
 
 def body(rhs, factors, diag_inv):
@@ -496,16 +672,16 @@
     pieces, chips, side = block // cols, n_row // 2, n_col // steps
     step_rows = rows_dev // CHUNKS
     dma = pltpu.SemaphoreType.DMA
-    vmem = pl.BlockSpec(memory_space=pltpu.VMEM)
     taken = pl.pallas_call(
         functools.partial(kernel, n_row, n_col, steps, block),
         out_shape=jax.ShapeDtypeStruct(rhs.shape, F32),
         in_specs=[pl.BlockSpec(memory_space=pl.ANY)] * 3,
-        out_specs=vmem,
+        out_specs=pl.BlockSpec(memory_space=pl.ANY),
         scratch_shapes=[
             pltpu.VMEM((block, width), F32),
             pltpu.VMEM(factors.shape, BF16),
             pltpu.VMEM((GATHER, n_row, step_rows, cols), BF16),
+            pltpu.VMEM(rhs.shape, F32),
             pltpu.VMEM((block, block), F32),
             pltpu.VMEM((block, block), BF16),
             pltpu.VMEM((block, block), BF16),
@@ -523,10 +699,11 @@
             pltpu.VMEM((CHUNKS, chips - 1, step_rows, width), BF16),
             pltpu.VMEM((CHUNKS, chips - 1, step_rows, width), BF16),
             dma, dma((2, CUTS)), dma((2, chips - 1, CUTS)), dma((n_row, 2, CUTS)), dma((n_row, CUTS)),
-            dma((steps, SUBS)), dma((steps, side, SUBS)), dma((steps, SUBS, pieces)), dma((steps, SUBS)), dma((SUBS,)),
+            dma((3, SUBS)), dma((steps, side, SUBS)), dma((steps, SUBS, pieces)), dma((side, 2 * (chips - 1), SUBS)),
+            dma((steps, SUBS)), dma((side, SUBS)), dma((steps, SUBS)), dma((SUBS,)), dma((SUBS,)),
             dma((SUBS,)), dma((n_row, SUBS)),
             dma((CHUNKS,)), dma((CHUNKS,)), dma((CHUNKS, chips - 1)), dma((CHUNKS, chips - 1)),
-            dma((GATHER, chips)), dma((GATHER, n_row)), dma((GATHER, chips)), dma((4,)),
+            dma((GATHER, chips)), dma((GATHER, n_row)), dma((GATHER, chips)), dma((4,)), dma((CHUNKS,)),
         ],
         compiler_params=pltpu.CompilerParams(
             collective_id=0, has_side_effects=True, vmem_limit_bytes=50 * 1024 * 1024

time: 67 us -> 64.6 us (0.964)
  Pallas kernels: 65.3 us -> 62.7 us
    pallas_call x1, Pallas kernels: 65.3 us -> 62.7 us  [body(): pl.pallas_call(functools.partial(kernel, n_row, n_col, steps, block), out...]
where the time goes in v2:
time: 64.6 us; the launch traced here: 64.2 us
  Pallas kernels  62.7 us (97%)
  other arithmetic  1.53 us (2%)
    pallas_call x1, Pallas kernels, body(): pl.pallas_call(functools.partial(kernel, n_row, n_col, steps, block), out...  62.7 us
    sub x1, other arithmetic, body(): return rhs - taken  1.53 us

profile of v2, /device:TPU:0, one launch (start us, length us, event | category | flops | bytes accessed | tf_op | source)
XLA Modules:
  0.0 64.2 jit_solution(8710629394494950270)
XLA Ops:
  0.0 0.0 copy-start
  0.0 62.7 %shard_map.37 = f32[4096,128]{1,0:T(8,128)S(1)} custom-call(f32[4096,128]{1,0:T(8,128)} %rhs_hbm.1, bf16[4096,512]{1,0:T(8,128)(2,1)} %factors_hbm.1, f32[4,512,512]{2,1,0:T(8,128)} %diag_ref.1), custom_call_target="tpu_custom_call" | custom-call | tf_op jit(solution)/shard_map/pallas_call | solution.py:675
  62.7 0.0 copy-done
  62.7 1.5 %sub.3 = f32[4096,128]{1,0:T(8,128)} subtract(f32[4096,128]{1,0:T(8,128)S(1)} %copy-done, f32[4096,128]{1,0:T(8,128)S(1)} %shard_map.37) | non-fusion elementwise | flops 524288 | bytes 6291456 | tf_op jit(solution)/shard_map/sub | solution.py:712
Async XLA Ops:
  0.0 62.7 %copy-start = (f32[4096,128]{1,0:T(8,128)S(1)}, f32[4096,128]{1,0:T(8,128)}, u32[]{:S(2)}) copy-start(f32[4096,128]{1,0:T(8,128)} %rhs_hbm.1) | copy-start | bytes 6291460

commit v3 on v2

--- a/solution.py
+++ b/solution.py
@@ -66,7 +66,7 @@
     base = zone * side
 
     diag_copy = pltpu.make_async_copy(diag_ref.at[zone], diag, diag_sem)
-    rhs_copy = pltpu.make_async_copy(rhs_hbm.at[pl.ds(0, block)], rhs_ref, load_sem.at[0])
+    rhs_copy = pltpu.make_async_copy(rhs_hbm, rhs_ref, load_sem.at[0])
     factors_copy = pltpu.make_async_copy(factors_hbm, factors_ref, load_sem.at[1])
     work_copy = pltpu.make_async_copy(rhs_hbm.at[pl.ds(0, block)], work, load_sem.at[2])
     panel_own = pltpu.make_async_copy(factors_hbm.at[pl.ds(0, block)], panel.at[row], load_sem.at[3])
@@ -112,17 +112,25 @@
     def needed(source):
         return jnp.logical_and(owner, source // pieces != zone)
 
-    def near_copy(h, c):
-        rows = cut(h, c)
-        return remote(factors_hbm.at[rows], panel.at[row, rows], f_send.at[h, c], f_recv.at[row, h, c], row=sibling)
+    def near_copy(mine, c):
+        rows = cut(core if mine else 1 - core, c)
+        there = f_recv.at[row, CUTS if mine else c]
+        return remote(factors_hbm.at[rows], panel.at[row, rows], f_send, there, row=sibling)
 
     def far_copy(source, d, c):
         piece = panel.at[source, cut(core, c)]
-        return remote(piece, piece, f_far.at[source % 2, d - 1, c], f_recv.at[source, core, c], row=far[d - 1])
-
-    def relay_copy(source, h, c):
-        piece = panel.at[source, cut(h, c)]
-        return remote(piece, piece, f_fwd.at[source, c], f_recv.at[source, h, c], row=sibling)
+        return remote(piece, piece, f_far.at[source % 2, d - 1], f_recv.at[source, c], row=far[d - 1])
+
+    def arriving(source, c):
+        piece = panel.at[source, cut(core, c)]
+        return remote(piece, piece, f_fwd.at[source], f_recv.at[source, c], row=sibling)
+
+    def relay_copy(source, c):
+        piece = panel.at[source, cut(core, c)]
+        return remote(piece, piece, f_fwd.at[source], f_recv.at[source, CUTS], row=sibling)
+
+    def half_block(source, h):
+        return panel.at[source, pl.ds(pl.multiple_of(h * half, half), half)]
 
     def far_sends(source):
         @pl.when(needed(source))
@@ -130,7 +138,7 @@
             @pl.when(source != row)
             def _():
                 for c in range(CUTS):
-                    relay_copy(source, core, c).wait_recv()
+                    arriving(source, c).wait_recv()
 
             for d in range(1, chips):
                 for c in range(CUTS):
@@ -152,12 +160,17 @@
 
     def extra_copy(g, d):
         return remote(
-            factors_hbm.at[span(CHUNKS - 1 - g)], extra.at[g, row], x_send.at[g, d], x_recv.at[g, row],
+            factors_hbm.at[span(CHUNKS - 1 - g)], extra.at[g, core, chip], x_send.at[g, d], x_recv.at[g, (chips - 1 if d == 0 else chips - 1 - d)],
             row=far[d - 1] if d else sibling,
         )
 
-    def extra_forward(g, source):
-        return remote(extra.at[g, source], extra.at[g, source], x_fwd.at[g, source // 2], x_recv.at[g, source], row=sibling)
+    def extra_arriving(g, d):
+        piece = extra.at[g, core, far[d - 1] // 2]
+        return remote(piece, piece, x_fwd.at[g, d - 1], x_recv.at[g, d - 1], row=sibling)
+
+    def extra_forward(g, d):
+        piece = extra.at[g, core, far[d - 1] // 2]
+        return remote(piece, piece, x_fwd.at[g, d - 1], x_recv.at[g, chips - 1], row=sibling)
 
     def extra_start(g, carry):
         for d in range(chips):
@@ -200,8 +213,8 @@
             @pl.when(is_far(source))
             def _():
                 for c in range(CUTS):
-                    relay_copy(source, core, c).wait_recv()
-                    relay_copy(source, core, c).start()
+                    arriving(source, c).wait_recv()
+                    relay_copy(source, c).start()
 
     def relay_back():
         def one(i, carry):
@@ -216,14 +229,14 @@
 
             @pl.when(source != row)
             def _():
-                for c in range(CUTS):
-                    relay_copy(source, 1 - core, c).wait_recv()
+                piece = half_block(source, 1 - core)
+                remote(piece, piece, f_fwd.at[source], f_recv.at[source, CUTS], row=sibling).wait_recv()
 
     def chain_copy(t, s):
         piece = solved.at[t, batch(s)]
         k = jnp.where(t == 0, 0, 1)
         return remote(
-            piece, piece, s_chain.at[k, s], s_recv.at[t, s], col=jnp.minimum(zone + 1, steps - 1) * side
+            piece, piece, s_chain.at[k], s_recv.at[t, s], col=jnp.minimum(zone + 1, steps - 1) * side
         )
 
     def chains(t):
@@ -231,45 +244,43 @@
 
     def arrival(j, s):
         piece = solved.at[j, batch(s)]
-        return remote(piece, piece, s_chain.at[0, s], s_recv.at[j, s], col=col)
+        return remote(piece, piece, s_chain.at[0], s_recv.at[j, s], col=col)
 
     def help_copy(z, s):
         piece = solved.at[zone, batch(s)]
-        return remote(piece, piece, s_help.at[z, s], s_recv.at[zone, s], col=z * side)
+        return remote(piece, piece, s_help.at[z], s_recv.at[zone, s], col=z * side)
 
     def help_last(z, s):
-        return remote(last.at[batch(s)], solved.at[zone, batch(s)], s_help.at[z, s], s_recv.at[zone, s], col=z * side)
+        return remote(last.at[batch(s)], solved.at[zone, batch(s)], s_help.at[z], s_recv.at[zone, s], col=z * side)
 
     def hint_copy(d, s):
-        return remote(last.at[batch(s)], last.at[batch(s)], s_hint.at[d, s], l_recv.at[s], col=base + d)
+        return remote(last.at[batch(s)], last.at[batch(s)], s_hint.at[d - 1], l_recv.at[s], col=base + d)
 
     def lane_last(s):
-        return remote(last.at[batch(s)], solved.at[zone, batch(s)], s_chain.at[0, s], s_recv.at[zone, s], col=lane)
+        return remote(last.at[batch(s)], solved.at[zone, batch(s)], s_chain.at[0], s_recv.at[zone, s], col=lane)
 
     def skip_last(s):
         target = jnp.maximum(zone - 2, 0) * side
-        return remote(last.at[batch(s)], solved.at[zone, batch(s)], s_chain.at[2, s], s_recv.at[zone, s], col=target)
-
-    def forwards(what, s):
+        return remote(last.at[batch(s)], solved.at[zone, batch(s)], s_chain.at[2], s_recv.at[zone, s], col=target)
+
+    def helps(z):
+        return jnp.logical_and(helper, jnp.logical_and(z > zone + 1, zone > 0))
+
+    def helps_back(z):
+        return jnp.logical_and(helper, z < zone - 2)
+
+    def forwards(s):
         for z in range(2, steps):
-            pl.when(jnp.logical_and(helper, jnp.logical_and(z > zone + 1, zone > 0)))(
-                lambda: what(help_copy(z, s))
-            )
-
-    def backwards(what, s):
+            pl.when(helps(z))(lambda: help_copy(z, s).start())
+
+    def backwards(s):
         for z in reversed(range(steps - 3)):
-            pl.when(jnp.logical_and(helper, z < zone - 2))(lambda: what(help_last(z, s)))
-        what(lane_last(s))
-
-    def begin(copy):
-        copy.start()
-
-    def finished(copy):
-        copy.wait_send()
+            pl.when(helps_back(z))(lambda: help_last(z, s).start())
+        lane_last(s).start()
 
     def side_copy(t, j, d, s):
         piece = solved.at[j, batch(s)]
-        return remote(piece, piece, s_side.at[t, d, s], s_recv.at[j, s], col=base + d)
+        return remote(piece, piece, s_side.at[t, d - 1], s_recv.at[j, s], col=base + d)
 
     def lends(t):
         return jnp.logical_and(zone == 0, t < steps)
@@ -277,7 +288,7 @@
     def row_copy(t, j, s, p):
         return remote(
             solved.at[j, batch(s), pl.ds(p * cols, cols)], gathered.at[core, batch(s, chip * width)],
-            s_row.at[t, s, p], g_recv.at[row, s], row=j * pieces + p,
+            s_row.at[t, p], g_recv.at[row, s], row=j * pieces + p,
         )
 
     def local_copy(j, s, p):
@@ -285,12 +296,10 @@
             solved.at[j, batch(s), pl.ds(p * cols, cols)], gathered.at[core, batch(s, chip * width)], g_local.at[s]
         )
 
-    def shares(t, j, s, what):
-        for p in range(pieces):
-            target = j * pieces + p
-            lent = jnp.logical_and(lends(t), target // 2 != chip)
-            sends = jnp.logical_and(target != row, jnp.logical_or(owner, jnp.logical_not(lent)))
-            pl.when(sends)(lambda: what(row_copy(t, j, s, p)))
+    def shares_with(t, j, p):
+        target = j * pieces + p
+        lent = jnp.logical_and(lends(t), target // 2 != chip)
+        return jnp.logical_and(target != row, jnp.logical_or(owner, jnp.logical_not(lent)))
 
     my_turn = jnp.where(row // pieces == 0, 0, steps - row // pieces)
     lender = jnp.logical_and(owner, lends(my_turn))
@@ -298,7 +307,7 @@
     def lend_copy(d, k, s):
         source = far[k // 2] // 2 * 2 + k % 2
         piece = gathered.at[k % 2, batch(s, (source // 2) * width)]
-        return remote(piece, piece, s_lend.at[d, k, s], g_recv.at[source, s], col=base + d)
+        return remote(piece, piece, s_lend.at[d - 1, k], g_recv.at[source, s], col=base + d)
 
     def lend(s):
         for k in range(2 * (chips - 1)):
@@ -311,6 +320,9 @@
     def has_sides(j):
         return jnp.logical_and(owner, jnp.logical_or(zone > 0, j < 2))
 
+    def sent(piece, sem):
+        remote(piece, piece, sem, sem, col=col).wait_send()
+
     def sides(t, j, s):
         for d in range(1, side):
             side_copy(t, j, d, s).start()
@@ -322,9 +334,9 @@
         def _():
             sides(t, j, s)
 
-        pl.when(t == zone)(lambda: forwards(begin, s))
-        shares(t, j, s, begin)
+        pl.when(t == zone)(lambda: forwards(s))
         for p in range(pieces):
+            pl.when(shares_with(t, j, p))(lambda: row_copy(t, j, s, p).start())
             pl.when(j * pieces + p == row)(lambda: local_copy(j, s, p).start())
 
     def update(j, s):
@@ -343,7 +355,7 @@
 
     def last_copy(s):
         target = jnp.where(zone > 0, zone - 1, 0) * side
-        return remote(last.at[batch(s)], solved.at[zone, batch(s)], s_last.at[s], s_recv.at[zone, s], col=target)
+        return remote(last.at[batch(s)], solved.at[zone, batch(s)], s_last, s_recv.at[zone, s], col=target)
 
     def solve_last(s):
         value = solve_up(state[batch(s)])
@@ -358,16 +370,17 @@
 
 
     def out_copy(m):
-        return pltpu.make_async_copy(taken.at[span(m)], out_ref.at[span(m)], out_sem.at[m])
+        return pltpu.make_async_copy(taken.at[span(m)], out_ref.at[span(m)], out_sem)
 
     def one_copy(m):
-        return remote(send1.at[m], recv1.at[m], one_send.at[m], one_recv.at[m], row=sibling)
+        return remote(send1.at[m], recv1.at[m], one_send.at[m % 2], one_recv.at[m], row=sibling)
 
     def two_copy(m, d):
         return remote(send2.at[m, d - 1], recv2.at[m, d - 1], two_send.at[m, d - 1], two_recv.at[m, d - 1], row=far[d - 1])
 
     def first(m, carry):
         send1[m] = dot_t(factors_ref[span(m)], gathered[1 - core]).astype(BF16)
+        pl.when(m > start + 1)(lambda: one_copy(m - 2).wait_send())
         one_copy(m).start()
         return carry
 
@@ -394,12 +407,12 @@
         for d in range(1, chips):
             two_copy(m, d).wait_recv()
             total = total + recv2[m, d - 1].astype(F32)
-        taken[span(m)] = total
+        taken[span(m)] = rhs_ref[span(m)] - total
         out_copy(m).start()
         return carry
 
     def finish(m, carry):
-        one_copy(m).wait_send()
+        pl.when(m > n_made - 3)(lambda: one_copy(m).wait_send())
         for d in range(1, chips):
             pl.when(m < CHUNKS - wants[d])(lambda: two_copy(m, d).wait_send())
         return carry
@@ -413,25 +426,27 @@
 
     def extra_hand_on(g, carry):
         for d in range(1, chips):
-            extra_forward(g, far[d - 1]).wait_recv()
-            extra_forward(g, far[d - 1]).start()
-        return carry
+            extra_arriving(g, d).wait_recv()
+            extra_forward(g, d).start()
+        return carry
+
+    def far_of(d):
+        return ((chip + d) % chips) * 2 + core
 
     def extra_product(g, carry):
         rows = span(CHUNKS - 1 - g)
         total = jnp.zeros((step_rows, width), F32)
+        theirs = extra.at[g, 1 - core]
         for d in range(n_row):
-            source = (row + d) % n_row
+            source = far_of(d) if d < chips else (far_of(d - chips) // 2) * 2 + 1 - core
             part_of = solved[source // pieces, :, pl.ds(pl.multiple_of((source % pieces) * cols, cols), cols)]
             if d == 0:
                 total = total + dot_t(factors_ref[rows], part_of)
             else:
-                @pl.when(source % 2 != core)
-                def _():
-                    extra_forward(g, source).wait_recv()
-
-                total = total + dot_t(extra[g, source], part_of)
-        taken[rows] = total
+                if d == chips:
+                    remote(theirs, theirs, x_fwd.at[g, 0], x_recv.at[g, chips - 1], row=sibling).wait_recv()
+                total = total + dot_t(extra[g, source % 2, source // 2], part_of)
+        taken[rows] = rhs_ref[rows] - total
         out_copy(CHUNKS - 1 - g).start()
         return carry
 
@@ -442,7 +457,7 @@
         @pl.when(g < n_extra)
         def _():
             for d in range(1, chips):
-                extra_forward(g, far[d - 1]).wait_send()
+                extra_forward(g, d).wait_send()
 
         return carry
 
@@ -496,9 +511,9 @@
     pl.semaphore_wait(barrier, n_row - 1 + jnp.where(owner, ends + side - 1, 1 + jnp.where(helper, beyond, 0)))
     @pl.when(sends_panel)
     def _():
-        for h in (1 - core, core):
+        for mine in (False, True):
             for c in range(CUTS):
-                near_copy(h, c).start()
+                near_copy(mine, c).start()
 
     @pl.when(owner)
     def _():
@@ -570,7 +585,7 @@
                 @pl.when(jnp.logical_and(t == steps - 1, zone > 1))
                 def _():
                     hint_copy(1, s).wait_recv()
-                    backwards(begin, s)
+                    backwards(s)
 
             batches(one)
             lax.fori_loop(head, jnp.where(i == 2, GATHER, head), extra_start, 0)
@@ -589,7 +604,7 @@
 
     @pl.when(owner)
     def _():
-        taken[pl.ds(0, block)] = rhs_ref[...] - state[...].T
+        taken[pl.ds(0, block)] = state[...].T
         for m in range(block // step_rows):
             out_copy(m).start()
 
@@ -599,20 +614,13 @@
 
     @pl.when(sends_panel)
     def _():
-        for h in range(2):
-            for c in range(CUTS):
-                near_copy(h, c).wait_send()
+        sent(panel.at[row], f_send)
 
     for source in (pair, pair + 1):
         @pl.when(needed(source))
         def _():
             for d in range(1, chips):
-                for c in range(CUTS):
-                    far_copy(source, d, c).wait_send()
-
-    def written(m, carry):
-        out_copy(m).wait()
-        return carry
+                sent(half_block(source, core), f_far.at[source % 2, d - 1])
 
     def drain(t, carry):
         j = slot(t)
@@ -622,46 +630,48 @@
 
             @pl.when(jnp.logical_and(is_far(source), t != zone))
             def _():
-                for c in range(CUTS):
-                    relay_copy(source, core, c).wait_send()
-
-        def one(s):
-            pl.when(chains(t))(lambda: chain_copy(t, s).wait_send())
-            pl.when(t == zone)(lambda: forwards(finished, s))
-
-            @pl.when(has_sides(j))
-            def _():
-                for d in range(1, side):
-                    side_copy(t, j, d, s).wait_send()
-
-            shares(t, j, s, finished)
-
-        batches(one)
+                sent(half_block(source, core), f_fwd.at[source])
+
+        pl.when(chains(t))(lambda: sent(solved.at[t], s_chain.at[jnp.where(t == 0, 0, 1)]))
+
+        @pl.when(t == zone)
+        def _():
+            for z in range(2, steps):
+                pl.when(helps(z))(lambda: sent(solved.at[zone], s_help.at[z]))
+
+        @pl.when(has_sides(j))
+        def _():
+            for d in range(1, side):
+                sent(solved.at[j], s_side.at[t, d - 1])
+
+        for p in range(pieces):
+            pl.when(shares_with(t, j, p))(lambda: sent(gathered.at[0, pl.ds(0, width)], s_row.at[t, p]))
+
         return carry
 
     lax.fori_loop(0, steps, drain, 0)
 
-    lax.fori_loop(0, CHUNKS, written, 0)
+    pltpu.make_async_copy(taken, out_ref, out_sem).wait()
 
     @pl.when(lender)
     def _():
         for d in range(1, side):
             for k in range(2 * (chips - 1)):
-                batches(lambda s: lend_copy(d, k, s).wait_send())
-
-    @pl.when(jnp.logical_and(owner, zone > 0))
-    def _():
-        batches(lambda s: last_copy(s).wait_send())
+                sent(gathered.at[0, pl.ds(0, width)], s_lend.at[d - 1, k])
+
+    pl.when(jnp.logical_and(owner, zone > 0))(lambda: sent(last, s_last))
 
     @pl.when(jnp.logical_and(owner, zone > 1))
     def _():
-        batches(lambda s: skip_last(s).wait_send())
+        sent(last, s_chain.at[2])
         for d in range(1, side):
-            batches(lambda s: hint_copy(d, s).wait_send())
+            sent(last, s_hint.at[d - 1])
 
     @pl.when(jnp.logical_and(jnp.logical_not(owner), zone > 1))
     def _():
-        batches(lambda s: backwards(finished, s))
+        sent(last, s_chain.at[0])
+        for z in range(steps - 3):
+            pl.when(helps_back(z))(lambda: sent(last, s_help.at[z]))
 
 
 def body(rhs, factors, diag_inv):
@@ -678,9 +688,9 @@
         in_specs=[pl.BlockSpec(memory_space=pl.ANY)] * 3,
         out_specs=pl.BlockSpec(memory_space=pl.ANY),
         scratch_shapes=[
-            pltpu.VMEM((block, width), F32),
+            pltpu.VMEM(rhs.shape, F32),
             pltpu.VMEM(factors.shape, BF16),
-            pltpu.VMEM((GATHER, n_row, step_rows, cols), BF16),
+            pltpu.VMEM((GATHER, 2, chips, step_rows, cols), BF16),
             pltpu.VMEM(rhs.shape, F32),
             pltpu.VMEM((block, block), F32),
             pltpu.VMEM((block, block), BF16),
@@ -698,18 +708,18 @@
             pltpu.VMEM((CHUNKS, step_rows, chips * width), F32),
             pltpu.VMEM((CHUNKS, chips - 1, step_rows, width), BF16),
             pltpu.VMEM((CHUNKS, chips - 1, step_rows, width), BF16),
-            dma, dma((2, CUTS)), dma((2, chips - 1, CUTS)), dma((n_row, 2, CUTS)), dma((n_row, CUTS)),
-            dma((3, SUBS)), dma((steps, side, SUBS)), dma((steps, SUBS, pieces)), dma((side, 2 * (chips - 1), SUBS)),
-            dma((steps, SUBS)), dma((side, SUBS)), dma((steps, SUBS)), dma((SUBS,)), dma((SUBS,)),
+            dma, dma, dma((2, chips - 1)), dma((n_row, CUTS + 1)), dma((n_row,)),
+            dma((3,)), dma((steps, side - 1)), dma((steps, pieces)), dma((side - 1, 2 * (chips - 1))),
+            dma((steps,)), dma((side - 1,)), dma((steps, SUBS)), dma((SUBS,)), dma,
             dma((SUBS,)), dma((n_row, SUBS)),
-            dma((CHUNKS,)), dma((CHUNKS,)), dma((CHUNKS, chips - 1)), dma((CHUNKS, chips - 1)),
-            dma((GATHER, chips)), dma((GATHER, n_row)), dma((GATHER, chips)), dma((4,)), dma((CHUNKS,)),
+            dma((2,)), dma((CHUNKS,)), dma((CHUNKS, chips - 1)), dma((CHUNKS, chips - 1)),
+            dma((GATHER, chips)), dma((GATHER, chips)), dma((GATHER, chips - 1)), dma((4,)), dma,
         ],
         compiler_params=pltpu.CompilerParams(
             collective_id=0, has_side_effects=True, vmem_limit_bytes=50 * 1024 * 1024
         ),
     )(rhs, factors, diag_inv)
-    return rhs - taken
+    return taken
 
 
 def solution(mesh):

time: 64.6 us -> 63.3 us (0.980)
  other arithmetic: 1.53 us -> 0 us
  local copies, waits for them, and re-layouts: 0.01 us -> 1.32 us
  Pallas kernels: 62.7 us -> 61.8 us
    sub x1 -> x0, other arithmetic: 1.53 us -> none  [body(): return rhs - taken]
    unnamed x2 -> x1, local copies, waits for them, and re-layouts: 0.01 us -> 1.32 us
    pallas_call x1, Pallas kernels: 62.7 us -> 61.8 us  [body(): pl.pallas_call(functools.partial(kernel, n_row, n_col, steps, block), out...]
where the time goes in v3:
time: 63.3 us; the launch traced here: 63.1 us
  Pallas kernels  61.8 us (98%)
  local copies, waits for them, and re-layouts  1.32 us (2%)
    pallas_call x1, Pallas kernels, body(): pl.pallas_call(functools.partial(kernel, n_row, n_col, steps, block), out...  61.8 us
    unnamed x1, local copies, waits for them, and re-layouts  1.32 us

profile of v3, /device:TPU:0, one launch (start us, length us, event | category | flops | bytes accessed | tf_op | source)
XLA Modules:
  0.0 63.1 jit_solution(3023860683145704209)
XLA Ops:
  0.0 61.8 %shard_map.37 = f32[4096,128]{1,0:T(8,128)S(1)} custom-call(f32[4096,128]{1,0:T(8,128)} %rhs_hbm.1, bf16[4096,512]{1,0:T(8,128)(2,1)} %factors_hbm.1, f32[4,512,512]{2,1,0:T(8,128)} %diag_ref.1), custom_call_target="tpu_custom_call" | custom-call | tf_op jit(solution)/shard_map/pallas_call | solution.py:685
  61.8 1.3 %copy.5 = f32[4096,128]{1,0:T(8,128)} copy(f32[4096,128]{1,0:T(8,128)S(1)} %shard_map.37) | data formatting | bytes 4194304

commit v4 on v3

--- a/solution.py
+++ b/solution.py
@@ -16,6 +16,7 @@
 GATHER = 4
 NEAR0, FAR0, NEAR1, FAR1, REST1 = 2, 3, 4, 4, 2
 HEAD0, HEAD1 = 2, 4
+AHEAD = 3
 
 
 def remote(src, dst, send_sem, recv_sem, **device):
@@ -46,7 +47,7 @@
     n_row, n_col, steps, block,
     rhs_hbm, factors_hbm, diag_ref, out_ref,
     rhs_ref, factors_ref, extra, taken,
-    diag, low_hi, low_lo, up_hi, up_lo, panel, solved, last, work, state, gathered,
+    diag, low, up, scale, panel, solved, last, work, state, gathered,
     send1, recv1, own1, send2, recv2,
     diag_sem, f_send, f_far, f_recv, f_fwd, s_chain, s_side, s_row, s_lend, s_help, s_hint, s_recv, l_recv, s_last, g_local, g_recv,
     one_send, one_recv, two_send, two_recv, x_send, x_recv, x_fwd, load_sem, out_sem,
@@ -184,21 +185,20 @@
         return pl.ds(pl.multiple_of(start + s * sub, sub), sub)
 
     def stacked(value):
-        high, low = split(value)
-        return high, jnp.concatenate([high, low])
-
-    def folded(both, more):
-        return both[:sub] + (both[sub:] + more)
+        return value.astype(BF16)
+
+    def folded(both):
+        return both
 
     def solve_low(value):
-        high, both = stacked(value)
-        top = folded(dot_t(both[:, :half], low_hi[:half, :half]), dot_t(high[:, :half], low_lo[:half, :half]))
-        return jnp.concatenate([top, folded(dot_t(both, low_hi[half:]), dot_t(high, low_lo[half:]))], axis=1)
+        both = stacked(value)
+        top = folded(dot_t(both[:, :half], low[:half, :half]))
+        return jnp.concatenate([top, folded(dot_t(both, low[half:]))], axis=1)
 
     def solve_up(value):
-        high, both = stacked(value)
-        end = folded(dot_t(both[:, half:], up_hi[half:, half:]), dot_t(high[:, half:], up_lo[half:, half:]))
-        return jnp.concatenate([folded(dot_t(both, up_hi[:half]), dot_t(high, up_lo[:half])), end], axis=1)
+        both = stacked(value)
+        end = folded(dot_t(both[:, half:], up[half:, half:]))
+        return value * scale[...] + jnp.concatenate([folded(dot_t(both, up[:half])), end], axis=1)
 
     def slot(t):
         return jnp.where(t <= zone, t, steps + zone - t)
@@ -385,10 +385,6 @@
         return carry
 
     def second(m, carry):
-        @pl.when(m + 1 < n_made)
-        def _():
-            first(m + 1, 0)
-
         own1[m] = dot_t(factors_ref[span(m)], gathered[core])
         one_copy(m).wait_recv()
         for d in range(1, chips):
@@ -399,6 +395,7 @@
                 send2[m, d - 1] = (own1[m, :, there] + recv1[m, :, there].astype(F32)).astype(BF16)
                 two_copy(m, d).start()
 
+        pl.when(m + 1 < n_made)(lambda: [first(m + 1, 0)] and None)
         return carry
 
     def third(m, carry):
@@ -461,10 +458,11 @@
 
         return carry
 
-    def first_products():
+    def loaded():
         factors_copy.wait()
         rhs_copy.wait()
 
+    def first_products():
         def arrive(s, carry):
             local_copy(0, s, 0).wait()
             for d in range(1, n_row):
@@ -491,8 +489,9 @@
         down = lax.broadcasted_iota(jnp.int32, (block, block), 0)
         across = lax.broadcasted_iota(jnp.int32, (block, block), 1)
         matrix = diag[...]
-        low_hi[...], low_lo[...] = split(jnp.where(down > across, matrix, 0.0))
-        up_hi[...], up_lo[...] = split(jnp.where(down <= across, matrix, 0.0))
+        low[...] = jnp.where(down > across, matrix, 0.0).astype(BF16)
+        up[...] = jnp.where(down < across, matrix, 0.0).astype(BF16)
+        scale[...] = jnp.sum(jnp.where(down == across, matrix, 0.0), axis=0, keepdims=True)
         state[...] = work[...].T
 
     def products():
@@ -574,6 +573,8 @@
 
     @pl.when(jnp.logical_not(owner))
     def _():
+        loaded()
+
         def hop(i, carry):
             t = jnp.where(put_off, (i + steps - 1) % steps, i)
             j = slot(t)
@@ -597,10 +598,14 @@
 
         lax.fori_loop(0, steps, each, 0)
 
+    pl.when(owner)(loaded)
+    done = jnp.where(jnp.logical_and(zone == 0, jnp.logical_not(jnp.logical_or(owner, sooner))), jnp.minimum(n_extra, AHEAD), 0)
+    lax.fori_loop(0, done, extra_hand_on, 0)
+    lax.fori_loop(0, done, extra_product, 0)
     pl.when(jnp.logical_not(sooner))(products)
-    lax.fori_loop(0, n_extra, extra_hand_on, 0)
+    lax.fori_loop(done, n_extra, extra_hand_on, 0)
     pl.when(jnp.logical_and(owner, zone == 0))(lambda: batches(solve_last))
-    lax.fori_loop(0, n_extra, extra_product, 0)
+    lax.fori_loop(done, n_extra, extra_product, 0)
 
     @pl.when(owner)
     def _():
@@ -695,8 +700,7 @@
             pltpu.VMEM((block, block), F32),
             pltpu.VMEM((block, block), BF16),
             pltpu.VMEM((block, block), BF16),
-            pltpu.VMEM((block, block), BF16),
-            pltpu.VMEM((block, block), BF16),
+            pltpu.VMEM((1, block), F32),
             pltpu.VMEM((n_row, block, cols), BF16),
             pltpu.VMEM((steps, width, block), BF16),
             pltpu.VMEM((width, block), BF16),

time: 63.3 us -> 63.1 us (level)
  no operation moved by 1% of the time
where the time goes in v4:
time: 63.1 us; the launch traced here: 63 us
  Pallas kernels  61.7 us (98%)
  local copies, waits for them, and re-layouts  1.32 us (2%)
    pallas_call x1, Pallas kernels, body(): pl.pallas_call(functools.partial(kernel, n_row, n_col, steps, block), out...  61.7 us
    unnamed x1, local copies, waits for them, and re-layouts  1.32 us

profile of v4, /device:TPU:0, one launch (start us, length us, event | category | flops | bytes accessed | tf_op | source)
XLA Modules:
  0.0 63.0 jit_solution(15591358201026132901)
XLA Ops:
  0.0 61.7 %shard_map.37 = f32[4096,128]{1,0:T(8,128)S(1)} custom-call(f32[4096,128]{1,0:T(8,128)} %rhs_hbm.1, bf16[4096,512]{1,0:T(8,128)(2,1)} %factors_hbm.1, f32[4,512,512]{2,1,0:T(8,128)} %diag_ref.1), custom_call_target="tpu_custom_call" | custom-call | tf_op jit(solution)/shard_map/pallas_call | solution.py:690
  61.7 1.3 %copy.5 = f32[4096,128]{1,0:T(8,128)} copy(f32[4096,128]{1,0:T(8,128)S(1)} %shard_map.37) | data formatting | bytes 4194304

commit v5 on v3

--- a/solution.py
+++ b/solution.py
@@ -16,6 +16,7 @@
 GATHER = 4
 NEAR0, FAR0, NEAR1, FAR1, REST1 = 2, 3, 4, 4, 2
 HEAD0, HEAD1 = 2, 4
+AHEAD = 3
 
 
 def remote(src, dst, send_sem, recv_sem, **device):
@@ -385,10 +386,6 @@
         return carry
 
     def second(m, carry):
-        @pl.when(m + 1 < n_made)
-        def _():
-            first(m + 1, 0)
-
         own1[m] = dot_t(factors_ref[span(m)], gathered[core])
         one_copy(m).wait_recv()
         for d in range(1, chips):
@@ -399,6 +396,7 @@
                 send2[m, d - 1] = (own1[m, :, there] + recv1[m, :, there].astype(F32)).astype(BF16)
                 two_copy(m, d).start()
 
+        pl.when(m + 1 < n_made)(lambda: [first(m + 1, 0)] and None)
         return carry
 
     def third(m, carry):
@@ -461,10 +459,11 @@
 
         return carry
 
-    def first_products():
+    def loaded():
         factors_copy.wait()
         rhs_copy.wait()
 
+    def first_products():
         def arrive(s, carry):
             local_copy(0, s, 0).wait()
             for d in range(1, n_row):
@@ -574,6 +573,8 @@
 
     @pl.when(jnp.logical_not(owner))
     def _():
+        loaded()
+
         def hop(i, carry):
             t = jnp.where(put_off, (i + steps - 1) % steps, i)
             j = slot(t)
@@ -597,10 +598,14 @@
 
         lax.fori_loop(0, steps, each, 0)
 
+    pl.when(owner)(loaded)
+    done = jnp.where(jnp.logical_and(zone == 0, jnp.logical_not(jnp.logical_or(owner, sooner))), jnp.minimum(n_extra, AHEAD), 0)
+    lax.fori_loop(0, done, extra_hand_on, 0)
+    lax.fori_loop(0, done, extra_product, 0)
     pl.when(jnp.logical_not(sooner))(products)
-    lax.fori_loop(0, n_extra, extra_hand_on, 0)
+    lax.fori_loop(done, n_extra, extra_hand_on, 0)
     pl.when(jnp.logical_and(owner, zone == 0))(lambda: batches(solve_last))
-    lax.fori_loop(0, n_extra, extra_product, 0)
+    lax.fori_loop(done, n_extra, extra_product, 0)
 
     @pl.when(owner)
     def _():

time: 63.3 us -> 63.3 us (level)
  no operation moved by 1% of the time
where the time goes in v5:
time: 63.3 us; the launch traced here: 63.1 us
  Pallas kernels  61.8 us (98%)
  local copies, waits for them, and re-layouts  1.32 us (2%)
    pallas_call x1, Pallas kernels, body(): pl.pallas_call(functools.partial(kernel, n_row, n_col, steps, block), out...  61.8 us
    unnamed x1, local copies, waits for them, and re-layouts  1.32 us

profile of v5, /device:TPU:0, one launch (start us, length us, event | category | flops | bytes accessed | tf_op | source)
XLA Modules:
  0.0 63.1 jit_solution(18328454121686336020)
XLA Ops:
  0.0 61.8 %shard_map.37 = f32[4096,128]{1,0:T(8,128)S(1)} custom-call(f32[4096,128]{1,0:T(8,128)} %rhs_hbm.1, bf16[4096,512]{1,0:T(8,128)(2,1)} %factors_hbm.1, f32[4,512,512]{2,1,0:T(8,128)} %diag_ref.1), custom_call_target="tpu_custom_call" | custom-call | tf_op jit(solution)/shard_map/pallas_call | solution.py:690
  61.8 1.3 %copy.5 = f32[4096,128]{1,0:T(8,128)} copy(f32[4096,128]{1,0:T(8,128)S(1)} %shard_map.37) | data formatting | bytes 4194304

commit v6 on v5

--- a/solution.py
+++ b/solution.py
@@ -12,7 +12,7 @@
 BF16 = jnp.bfloat16
 CHUNKS = 8
 SUBS = 2
-CUTS = 2
+CUTS = 1
 GATHER = 4
 NEAR0, FAR0, NEAR1, FAR1, REST1 = 2, 3, 4, 4, 2
 HEAD0, HEAD1 = 2, 4

time: 63.3 us -> 63.4 us (level)
  no operation moved by 1% of the time
where the time goes in v6:
time: 63.4 us; the launch traced here: 63.3 us
  Pallas kernels  61.9 us (98%)
  local copies, waits for them, and re-layouts  1.32 us (2%)
    pallas_call x1, Pallas kernels, body(): pl.pallas_call(functools.partial(kernel, n_row, n_col, steps, block), out...  61.9 us
    unnamed x1, local copies, waits for them, and re-layouts  1.32 us

profile of v6, /device:TPU:0, one launch (start us, length us, event | category | flops | bytes accessed | tf_op | source)
XLA Modules:
  0.0 63.3 jit_solution(5970860846181825457)
XLA Ops:
  0.0 61.9 %shard_map.37 = f32[4096,128]{1,0:T(8,128)S(1)} custom-call(f32[4096,128]{1,0:T(8,128)} %rhs_hbm.1, bf16[4096,512]{1,0:T(8,128)(2,1)} %factors_hbm.1, f32[4,512,512]{2,1,0:T(8,128)} %diag_ref.1), custom_call_target="tpu_custom_call" | custom-call | tf_op jit(solution)/shard_map/pallas_call | solution.py:690
  61.9 1.3 %copy.5 = f32[4096,128]{1,0:T(8,128)} copy(f32[4096,128]{1,0:T(8,128)S(1)} %shard_map.37) | data formatting | bytes 4194304
